TPU v7x, 32 devices: a whole 2x2x4 slice. The times are simulated.
32 devices in a mesh: mass: 8 (over z, y), prot: 4 (over x, core).
Axes of the slice: x: 2, y: 2, z: 4, core: 2. Of those that a mesh axis runs over, the one named last changes fastest.
Arguments:
- spectra: bfloat16 [32768, 512], P(('mass', 'prot')), may hold values from -6 to 6
- peptides: bfloat16 [32768, 512], P(('mass', 'prot')), may hold values from -6 to 6
- destination: int32 [32768], P(('mass', 'prot')), may hold values from 0 to 32767, as said below
- band: int32 [128, 6], P(('mass', 'prot')), may hold values from 0 to 7, as said below
- positive: int32 [32768], P(('mass', 'prot')), may hold values from 0 to 1535
- logit_scale: float32 [1], replicated, may hold values from 1 to 2
- logit_bias: float32 [1], replicated, may hold values from -3 to -1
Outputs:
- spectra_grad: bfloat16 [32768, 512], P(('mass', 'prot'))
- peptide_grad: bfloat16 [32768, 512], P(('mass', 'prot'))
Inputs may be any that keep to these rules, and one draw needn't show every extreme that they name: destination is a permutation. A peptide of device s fills a row of the block of 1024 table rows of some device o with the same placement; every device sends between 1 and 63 peptides to every device, and exactly 63 to some in every draw. `band`: the 6 entries of a row are distinct. The first device's blocks never name entries below 2, the last device's never entries at or above 6.
All inputs are finite; a program needn't handle non-finite values.
Results may differ from a plain program's by a relative error of at most 0.0065.
Values may be sent and summed in bfloat16 or wider, within the bound.
No kernel may reach another device: no remote copies, remote signals or barrier semaphores. Data moves between devices by JAX's collectives and lax.ppermute only.
A program may use at most 64 MiB of HBM per device.

v0:
```python
import math

import jax
import jax.numpy as jnp
from jax import lax
from jax.sharding import PartitionSpec as P

TILE_ROWS = 256
EDGE = 2
NB = 6
TILE_DEV = 4
SB = 4


def padded(value, sides, width):
    for axis, dim in sides:
        peers, length = (lax.axis_size(axis), value.shape[dim])
        up = [(i, (i + 1) % peers) for i in range(peers - 1)]
        down = [(j, i) for i, j in up]
        last = lax.slice_in_dim(value, length - width, length, axis=dim)
        leading = lax.slice_in_dim(value, 0, width, axis=dim)
        before = lax.ppermute(last, axis, up)
        after = lax.ppermute(leading, axis, down)
        value = jnp.concatenate([before, value, after], axis=dim)
    return value


def shifted(value, axis, steps):
    count = lax.axis_size(axis)
    leading, last = (max(0, -steps), min(count, count - steps))
    return lax.ppermute(value, axis, [(source, source + steps) for source in range(leading, last)])


def body(spectra, peptides, destination, band, positive, logit_scale, logit_bias):
    n_mass = lax.axis_size("mass")
    n_prot = lax.axis_size("prot")
    devices = n_mass * n_prot
    pep_rows, width = peptides.shape
    capacity = 2 * (pep_rows // devices) - 1
    owners = destination // pep_rows
    local_slot = destination - owners * pep_rows
    ordering = jnp.argsort(owners, stable=True)
    sorted_owners = owners[ordering]
    group_start = jnp.searchsorted(sorted_owners, sorted_owners, side="left")
    ranks = (
        jnp.zeros((pep_rows,), jnp.int32)
        .at[ordering]
        .set(jnp.arange(pep_rows, dtype=jnp.int32) - group_start)
    )
    position = owners * capacity + ranks
    send_rows = jnp.zeros((devices * capacity, width), jnp.bfloat16).at[position].set(peptides)
    send_slots = jnp.zeros((devices * capacity,), jnp.int32).at[position].set(local_slot + 1)
    send_rows = send_rows.reshape(n_mass, n_prot, capacity, width)
    send_slots = send_slots.reshape(n_mass, n_prot, capacity)
    got_rows, got_slots = (
        lax.all_to_all(
            lax.all_to_all(send_rows, "mass", split_axis=0, concat_axis=0, tiled=True),
            "prot",
            split_axis=1,
            concat_axis=1,
            tiled=True,
        ),
        lax.all_to_all(
            lax.all_to_all(send_slots, "mass", split_axis=0, concat_axis=0, tiled=True),
            "prot",
            split_axis=1,
            concat_axis=1,
            tiled=True,
        ),
    )
    got_rows = got_rows.reshape(devices * capacity, width)
    got_slots = got_slots.reshape(devices * capacity)
    target = jnp.where(got_slots > 0, got_slots - 1, pep_rows)
    table = jnp.zeros((pep_rows + 1, width), jnp.bfloat16).at[target].set(got_rows)[:pep_rows]
    own_tiles = table.reshape(TILE_DEV, TILE_ROWS, width)
    extended = padded(own_tiles, ((("mass", "prot"), 0),), EDGE)
    scaling = logit_scale[0] / math.sqrt(width)
    offset = logit_bias[0]
    spec_blocks = spectra.reshape(SB, TILE_ROWS, width)
    pos_blocks = positive.reshape(SB, TILE_ROWS)
    column_ids = jnp.arange(NB * TILE_ROWS, dtype=jnp.int32)

    def block_step(ext_grad, inputs):
        spec_block, chosen, wanted = inputs
        columns = extended[chosen].reshape(NB * TILE_ROWS, width)
        logits = (
            scaling
            * jnp.einsum("rd,cd->rc", spec_block, columns, preferred_element_type=jnp.float32)
            + offset
        )
        labels = (column_ids[None, :] == wanted[:, None]).astype(jnp.float32)
        weights = (jax.nn.sigmoid(logits) - labels).astype(jnp.bfloat16)
        spec_grad = (
            scaling * jnp.dot(weights, columns, preferred_element_type=jnp.float32)
        ).astype(jnp.bfloat16)
        tile_grad = scaling * jnp.einsum(
            "rc,rd->cd", weights, spec_block, preferred_element_type=jnp.float32
        )
        ext_grad = ext_grad.at[chosen].add(tile_grad.reshape(NB, TILE_ROWS, width))
        return (ext_grad, spec_grad)

    grad_start = jnp.zeros((TILE_DEV + 2 * EDGE, TILE_ROWS, width), jnp.float32)
    ext_grad, spec_grads = lax.scan(block_step, grad_start, (spec_blocks, band, pos_blocks))
    from_right = shifted(ext_grad[:EDGE].astype(jnp.bfloat16), ("mass", "prot"), -1).astype(
        jnp.float32
    )
    from_left = shifted(
        ext_grad[EDGE + TILE_DEV :].astype(jnp.bfloat16), ("mass", "prot"), 1
    ).astype(jnp.float32)
    own_grad = ext_grad[EDGE : EDGE + TILE_DEV]
    own_grad = own_grad.at[:EDGE].add(from_left)
    own_grad = own_grad.at[TILE_DEV - EDGE :].add(from_right)
    own_flat = jnp.concatenate(
        [
            own_grad.reshape(pep_rows, width).astype(jnp.bfloat16),
            jnp.zeros((1, width), jnp.bfloat16),
        ],
        0,
    )
    back_rows = own_flat[target].reshape(n_mass, n_prot, capacity, width)
    returned = lax.all_to_all(
        lax.all_to_all(back_rows, "mass", split_axis=0, concat_axis=0, tiled=True),
        "prot",
        split_axis=1,
        concat_axis=1,
        tiled=True,
    )
    returned = returned.reshape(devices * capacity, width)
    peptide_grad = returned[position]
    return (spec_grads.reshape(SB * TILE_ROWS, width), peptide_grad)


def solution(mesh):
    in_specs = (
        P(("mass", "prot"), None),
        P(("mass", "prot"), None),
        P(("mass", "prot")),
        P(("mass", "prot"), None),
        P(("mass", "prot")),
        P(),
        P(),
    )
    out_specs = (P(("mass", "prot"), None), P(("mass", "prot"), None))
    return jax.shard_map(body, mesh=mesh, in_specs=in_specs, out_specs=out_specs, check_vma=False)
```

profile of v0, /device:TPU:0, one launch (start us, length us, event | category | flops | bytes accessed | tf_op | source)
XLA Modules:
  0.0 398.4 jit_solution(18336134830479561871)
XLA Ops:
  1.3 4.4 %sort.17 = (s32[1024]{0:T(1024)}, s32[1024]{0:T(1024)S(1)}) sort(s32[1024]{0:T(1024)S(1)} %add_select_fusion.1, s32[1024]{0:T(1024)S(1)} %iota.10), dimensions={0}, to_apply=%region_0.1 | sort | flops 10240 | bytes 16384 | tf_op jit(solution)/shard_map/jit(argsort)/sort | solution.py:42
  5.7 4.5 %gather_fusion.2 = s32[1024]{0:T(1024)S(1)} fusion(s32[1024]{0:T(1024)S(1)} %add_select_fusion.1, s32[1024]{0:T(1024)S(1)} %get-tuple-element.221), kind=kCustom, calls=%fused_computation.2 | custom fusion | bytes 12288 | tf_op jit(solution)/shard_map/gather | solution.py:43
  10.3 50.7 %while.41 = (s32[]{:T(128)}, u32[1024]{0:T(1024)S(1)}, u32[1024]{0:T(1024)S(1)}, s32[1024]{0:T(1024)S(1)}, s32[]{:T(128)}, /*index=5*/s32[]{:T(128)}, s32[]{}) while((s32[]{:T(128)}, u32[1024]{0:T(1024)S(1)}, u32[1024]{0:T(1024)S(1)}, s32[1024]{0:T(1024)S(1)}, s32[]{:T(128)}, /*index=5*/s32[]{:T(128)}, s32[]{}) %tuple.69), condition=%wide.region_2.3_spmd.clone, body=%wide.region_1.2_spmd.clone.sunk | while | flops 19460 | bytes 67685 | solution.py:44
  10.3 4.5 %gather_fusion.1 = s32[1024]{0:T(1024)S(1)} fusion(s32[1024]{0:T(1024)S(1)} %get-tuple-element.324, u32[1024]{0:T(1024)S(1)} %broadcast_clamp_fusion.4), kind=kCustom, calls=%fused_computation.clone.clone.1 | custom fusion | bytes 12288 | tf_op jit(solution)/shard_map/jit(searchsorted)/jit(_searchsorted_scan_impl)/vmap(jit(_searchsorted_scan_impl))/while/body/eval_jaxpr/gather | solution.py:44
  14.9 4.5 %gather_fusion.1 = s32[1024]{0:T(1024)S(1)} fusion(s32[1024]{0:T(1024)S(1)} %get-tuple-element.324, u32[1024]{0:T(1024)S(1)} %broadcast_clamp_fusion.4), kind=kCustom, calls=%fused_computation.clone.clone.1 | custom fusion | bytes 12288 | tf_op jit(solution)/shard_map/jit(searchsorted)/jit(_searchsorted_scan_impl)/vmap(jit(_searchsorted_scan_impl))/while/body/eval_jaxpr/gather | solution.py:44
  19.5 4.5 %gather_fusion.1 = s32[1024]{0:T(1024)S(1)} fusion(s32[1024]{0:T(1024)S(1)} %get-tuple-element.324, u32[1024]{0:T(1024)S(1)} %broadcast_clamp_fusion.4), kind=kCustom, calls=%fused_computation.clone.clone.1 | custom fusion | bytes 12288 | tf_op jit(solution)/shard_map/jit(searchsorted)/jit(_searchsorted_scan_impl)/vmap(jit(_searchsorted_scan_impl))/while/body/eval_jaxpr/gather | solution.py:44
  24.1 4.5 %gather_fusion.1 = s32[1024]{0:T(1024)S(1)} fusion(s32[1024]{0:T(1024)S(1)} %get-tuple-element.324, u32[1024]{0:T(1024)S(1)} %broadcast_clamp_fusion.4), kind=kCustom, calls=%fused_computation.clone.clone.1 | custom fusion | bytes 12288 | tf_op jit(solution)/shard_map/jit(searchsorted)/jit(_searchsorted_scan_impl)/vmap(jit(_searchsorted_scan_impl))/while/body/eval_jaxpr/gather | solution.py:44
  28.7 4.5 %gather_fusion.1 = s32[1024]{0:T(1024)S(1)} fusion(s32[1024]{0:T(1024)S(1)} %get-tuple-element.324, u32[1024]{0:T(1024)S(1)} %broadcast_clamp_fusion.4), kind=kCustom, calls=%fused_computation.clone.clone.1 | custom fusion | bytes 12288 | tf_op jit(solution)/shard_map/jit(searchsorted)/jit(_searchsorted_scan_impl)/vmap(jit(_searchsorted_scan_impl))/while/body/eval_jaxpr/gather | solution.py:44
  33.3 4.5 %gather_fusion.1 = s32[1024]{0:T(1024)S(1)} fusion(s32[1024]{0:T(1024)S(1)} %get-tuple-element.324, u32[1024]{0:T(1024)S(1)} %broadcast_clamp_fusion.4), kind=kCustom, calls=%fused_computation.clone.clone.1 | custom fusion | bytes 12288 | tf_op jit(solution)/shard_map/jit(searchsorted)/jit(_searchsorted_scan_impl)/vmap(jit(_searchsorted_scan_impl))/while/body/eval_jaxpr/gather | solution.py:44
  38.0 4.5 %gather_fusion.1 = s32[1024]{0:T(1024)S(1)} fusion(s32[1024]{0:T(1024)S(1)} %get-tuple-element.324, u32[1024]{0:T(1024)S(1)} %broadcast_clamp_fusion.4), kind=kCustom, calls=%fused_computation.clone.clone.1 | custom fusion | bytes 12288 | tf_op jit(solution)/shard_map/jit(searchsorted)/jit(_searchsorted_scan_impl)/vmap(jit(_searchsorted_scan_impl))/while/body/eval_jaxpr/gather | solution.py:44
  42.6 4.5 %gather_fusion.1 = s32[1024]{0:T(1024)S(1)} fusion(s32[1024]{0:T(1024)S(1)} %get-tuple-element.324, u32[1024]{0:T(1024)S(1)} %broadcast_clamp_fusion.4), kind=kCustom, calls=%fused_computation.clone.clone.1 | custom fusion | bytes 12288 | tf_op jit(solution)/shard_map/jit(searchsorted)/jit(_searchsorted_scan_impl)/vmap(jit(_searchsorted_scan_impl))/while/body/eval_jaxpr/gather | solution.py:44
  47.2 4.5 %gather_fusion.1 = s32[1024]{0:T(1024)S(1)} fusion(s32[1024]{0:T(1024)S(1)} %get-tuple-element.324, u32[1024]{0:T(1024)S(1)} %broadcast_clamp_fusion.4), kind=kCustom, calls=%fused_computation.clone.clone.1 | custom fusion | bytes 12288 | tf_op jit(solution)/shard_map/jit(searchsorted)/jit(_searchsorted_scan_impl)/vmap(jit(_searchsorted_scan_impl))/while/body/eval_jaxpr/gather | solution.py:44
  51.8 4.5 %gather_fusion.1 = s32[1024]{0:T(1024)S(1)} fusion(s32[1024]{0:T(1024)S(1)} %get-tuple-element.324, u32[1024]{0:T(1024)S(1)} %broadcast_clamp_fusion.4), kind=kCustom, calls=%fused_computation.clone.clone.1 | custom fusion | bytes 12288 | tf_op jit(solution)/shard_map/jit(searchsorted)/jit(_searchsorted_scan_impl)/vmap(jit(_searchsorted_scan_impl))/while/body/eval_jaxpr/gather | solution.py:44
  56.4 4.5 %gather_fusion.1 = s32[1024]{0:T(1024)S(1)} fusion(s32[1024]{0:T(1024)S(1)} %get-tuple-element.324, u32[1024]{0:T(1024)S(1)} %broadcast_clamp_fusion.4), kind=kCustom, calls=%fused_computation.clone.clone.1 | custom fusion | bytes 12288 | tf_op jit(solution)/shard_map/jit(searchsorted)/jit(_searchsorted_scan_impl)/vmap(jit(_searchsorted_scan_impl))/while/body/eval_jaxpr/gather | solution.py:44
  61.0 4.3 %scatter_custom_fusion.1 = s32[1024]{0:T(1024)S(1)} fusion(s32[1024]{0:T(1024)S(1)} %get-tuple-element.222, s32[1024]{0:T(1024)S(1)} %convert_subtract_fusion, s32[]{:T(128)} %copy.49), kind=kCustom, calls=%fused_computation.67 | custom fusion | bytes 4100 | tf_op jit(solution)/shard_map/scatter | solution.py:48
  65.4 4.3 %scatter_custom_fusion.2 = s32[2016]{0:T(1024)S(1)} fusion(s32[1024]{0:T(1024)S(1)} %get-tuple-element.215, s32[1024]{0:T(1024)S(1)} %get-tuple-element.220, s32[]{:T(128)} %copy.49), kind=kCustom, calls=%fused_computation.62 | custom fusion | bytes 8068 | tf_op jit(solution)/shard_map/scatter | solution.py:52
  70.5 7.3 %all-to-all-start = ((s32[8,1,252]{2,1,0:T(1,128)}), s32[8,1,252]{2,1,0:T(1,128)S(1)}, u32[]{:S(2)}, u32[]{:S(2)}) async-start(s32[8,1,252]{2,1,0:T(1,128)} %reshape.285), calls=%async_computation | async-start | bytes 16384 | tf_op jit(solution)/shard_map/all_to_all | solution.py:64
  77.8 7.2 %scatter_custom_fusion.3 = bf16[2016,512]{1,0:T(8,128)(2,1)} fusion(s32[1024]{0:T(1024)S(1)} %get-tuple-element.215, bf16[1024,512]{1,0:T(8,128)(2,1)} %param.16, bf16[]{:T(256)} %constant.133.clone.1), kind=kCustom, calls=%fused_computation.45 | custom fusion | bytes 2064896 | tf_op jit(solution)/shard_map/scatter | solution.py:51
  85.0 1.9 reshape.174
  86.8 3.0 copy.17
  89.8 6.0 %all-to-all-start.2 = ((bf16[8,4,63,512]{3,1,2,0:T(4,128)(2,1)}), bf16[8,4,63,512]{3,1,2,0:T(4,128)(2,1)S(1)}, u32[]{:S(2)}, u32[]{:S(2)}) async-start(bf16[8,4,63,512]{3,1,2,0:T(4,128)(2,1)} %copy.17), calls=%async_computation.2 | async-start | bytes 4128768 | tf_op jit(solution)/shard_map/all_to_all | solution.py:57
  97.7 45.0 %all-to-all-done.2 = bf16[8,4,63,512]{3,1,2,0:T(4,128)(2,1)S(1)} async-done(((bf16[8,4,63,512]{3,1,2,0:T(4,128)(2,1)}), bf16[8,4,63,512]{3,1,2,0:T(4,128)(2,1)S(1)}, u32[]{:S(2)}, u32[]{:S(2)}) %all-to-all-start.2) | async-done | bytes 2064416 | tf_op jit(solution)/shard_map/all_to_all | solution.py:57
  142.8 3.2 all-to-all-start.1
  146.0 1.7 copy.18
  147.7 2.1 all-to-all-done.1
  149.8 4.6 %all-to-all-start.3 = ((bf16[8,4,63,512]{3,0,2,1:T(8,128)(2,1)}), bf16[8,4,63,512]{3,0,2,1:T(8,128)(2,1)}, u32[]{:S(2)}, u32[]{:S(2)}) async-start(bf16[8,4,63,512]{3,0,2,1:T(8,128)(2,1)} %copy.18), calls=%async_computation.3 | async-start | bytes 4128768 | tf_op jit(solution)/shard_map/all_to_all | solution.py:56
  155.3 24.3 %all-to-all-done.3 = bf16[8,4,63,512]{3,0,2,1:T(8,128)(2,1)} async-done(((bf16[8,4,63,512]{3,0,2,1:T(8,128)(2,1)}), bf16[8,4,63,512]{3,0,2,1:T(8,128)(2,1)}, u32[]{:S(2)}, u32[]{:S(2)}) %all-to-all-start.3) | async-done | bytes 2064416 | tf_op jit(solution)/shard_map/all_to_all | solution.py:56
  179.6 2.2 copy.19
  181.9 1.7 reshape.257
  183.5 11.1 %scatter_custom_fusion.4 = bf16[1025,512]{1,0:T(8,128)(2,1)S(1)} fusion(s32[2016]{0:T(1024)S(1)} %bitcast.74, bf16[2016,512]{1,0:T(8,128)(2,1)} %reshape.257, bf16[]{:T(256)} %constant.133.clone.1), kind=kCustom, calls=%fused_computation.47 | custom fusion | bytes 1050112 | tf_op jit(solution)/shard_map/scatter | solution.py:74
  194.7 1.3 collective-permute-start.1
  196.0 3.1 collective-permute-start
  200.5 1.6 pad_maximum_fusion
  202.1 2.5 broadcast_in_dim.55
  204.6 63.5 %while.40 = (s32[]{:T(128)}, f32[8,256,512]{2,1,0:T(8,128)}, bf16[4,256,512]{2,1,0:T(8,128)(2,1)}, s32[4,6]{1,0:T(4,128)}, f32[]{:T(128)}, /*index=5*/bf16[4,256...) while((s32[]{:T(128)}, f32[8,256,512]{2,1,0:T(8,128)}, ...), condition=%wide.region_9.10_spmd.clone, body=%wide.region_7.9_spmd.clone.sunk | while | flops 1213334528 | bytes 22029560 | solution.py:103
  205.3 2.2 gather_fusion
  207.5 2.4 fusion.53
  211.2 1.6 convolution_multiply_fusion.4
  212.8 7.7 %scatter_fusion = f32[8,256,512]{2,1,0:T(8,128)} fusion(f32[8,256,512]{2,1,0:T(8,128)} %get-tuple-element.339, s32[6]{0:T(128)S(1)} %fusion.52, f32[6,256,512]{2,1,0:T(8,128)S(1)} %bitcast.66), kind=kCustom, calls=%fused_computation.5.clone.clone.1 | custom fusion | flops 786432 | bytes 9437208 | tf_op jit(solution)/shard_map/while/body/eval_jaxpr/scatter-add | solution.py:99
  221.1 2.2 gather_fusion
  223.4 2.4 fusion.53
  227.1 1.6 convolution_multiply_fusion.4
  228.7 7.7 %scatter_fusion = f32[8,256,512]{2,1,0:T(8,128)} fusion(f32[8,256,512]{2,1,0:T(8,128)} %get-tuple-element.339, s32[6]{0:T(128)S(1)} %fusion.52, f32[6,256,512]{2,1,0:T(8,128)S(1)} %bitcast.66), kind=kCustom, calls=%fused_computation.5.clone.clone.1 | custom fusion | flops 786432 | bytes 9437208 | tf_op jit(solution)/shard_map/while/body/eval_jaxpr/scatter-add | solution.py:99
  237.0 2.2 gather_fusion
  239.3 2.4 fusion.53
  243.0 1.6 convolution_multiply_fusion.4
  244.5 7.6 %scatter_fusion = f32[8,256,512]{2,1,0:T(8,128)} fusion(f32[8,256,512]{2,1,0:T(8,128)} %get-tuple-element.339, s32[6]{0:T(128)S(1)} %fusion.52, f32[6,256,512]{2,1,0:T(8,128)S(1)} %bitcast.66), kind=kCustom, calls=%fused_computation.5.clone.clone.1 | custom fusion | flops 786432 | bytes 9437208 | tf_op jit(solution)/shard_map/while/body/eval_jaxpr/scatter-add | solution.py:99
  252.9 2.2 gather_fusion
  255.1 2.4 fusion.53
  257.5 1.3 fusion.54
  258.8 1.6 convolution_multiply_fusion.4
  260.4 7.7 %scatter_fusion = f32[8,256,512]{2,1,0:T(8,128)} fusion(f32[8,256,512]{2,1,0:T(8,128)} %get-tuple-element.339, s32[6]{0:T(128)S(1)} %fusion.52, f32[6,256,512]{2,1,0:T(8,128)S(1)} %bitcast.66), kind=kCustom, calls=%fused_computation.5.clone.clone.1 | custom fusion | flops 786432 | bytes 9437208 | tf_op jit(solution)/shard_map/while/body/eval_jaxpr/scatter-add | solution.py:99
  268.0 2.6 convert.4
  270.7 12.0 %collective-permute-start.2 = (bf16[2,256,512]{2,1,0:T(8,128)(2,1)S(1)}, bf16[2,256,512]{2,1,0:T(8,128)(2,1)S(1)}, u32[]{:S(2)}, u32[]{:S(2)}) collective-permute-start(bf16[2,256,512]{2,1,0:T(8,128)(2,1)S(1)} %get-tuple-element.217), channel_id=1, source_target_pairs={{0,1},{1,2},{2,3},{3,4},{4,5},{5,6},{6,7},{7,8},{8,9},{9,10},{10,1... | collective-permute-start | bytes 1572872 | tf_op jit(solution)/shard_map/ppermute | solution.py:31
  282.7 1.3 collective-permute-start.3
  284.4 3.9 collective-permute-done.3
  288.8 9.2 %gather_fusion.3 = bf16[2016,512]{1,0:T(8,128)(2,1)} fusion(bf16[1025,512]{1,0:T(8,128)(2,1)S(1)} %concatenate.11, s32[2048]{0:T(1024)S(1)} %pad_clamp_fusion.1), kind=kCustom, calls=%fused_computation.3 | custom fusion | bytes 4136832 | tf_op jit(solution)/shard_map/gather | solution.py:120
  298.0 1.9 reshape.179
  299.9 1.6 copy.20
  301.5 59.7 %all_to_all.30 = bf16[8,4,63,512]{3,1,2,0:T(4,128)(2,1)S(1)} all-to-all(bf16[8,4,63,512]{3,1,2,0:T(4,128)(2,1)S(1)} %copy.20), channel_id=1, replica_groups=mesh['mass'=8,'prot'=4] {'mass'}, dimensions={0} | all-to-all | bytes 4128768 | tf_op jit(solution)/shard_map/all_to_all | solution.py:122
  361.6 27.8 %all_to_all.31 = bf16[8,4,63,512]{3,0,2,1:T(8,128)(2,1)S(1)} all-to-all(bf16[8,4,63,512]{3,0,2,1:T(8,128)(2,1)S(1)} %copy.21), channel_id=1, replica_groups=mesh['mass'=8,'prot'=4] {'prot'}, dimensions={1} | all-to-all | bytes 4128768 | tf_op jit(solution)/shard_map/all_to_all | solution.py:121
  389.4 2.0 copy.22
  391.4 1.9 reshape.180
  393.3 5.1 %gather_fusion.4 = bf16[1024,512]{1,0:T(8,128)(2,1)} fusion(bf16[2016,512]{1,0:T(8,128)(2,1)S(1)} %reshape.180, s32[1024]{0:T(1024)S(1)} %get-tuple-element.214), kind=kCustom, calls=%fused_computation.4 | custom fusion | bytes 2101248 | tf_op jit(solution)/shard_map/gather | solution.py:129
  (101 shorter events, 13.6 us)
Async XLA Ops:
  10.2 55.1 %copy-start.1 = (s32[1024]{0:T(1024)S(1)}, s32[1024]{0:T(1024)}, u32[]{:S(2)}) copy-start(s32[1024]{0:T(1024)} %param.17) | copy-start | bytes 12292
  70.5 19.3 %all-to-all-start = ((s32[8,1,252]{2,1,0:T(1,128)}), s32[8,1,252]{2,1,0:T(1,128)S(1)}, u32[]{:S(2)}, u32[]{:S(2)}) async-start(s32[8,1,252]{2,1,0:T(1,128)} %reshape.285), calls=%async_computation | async-start | bytes 16384 | tf_op jit(solution)/shard_map/all_to_all | solution.py:64
  89.8 53.0 %all-to-all-start.2 = ((bf16[8,4,63,512]{3,1,2,0:T(4,128)(2,1)}), bf16[8,4,63,512]{3,1,2,0:T(4,128)(2,1)S(1)}, u32[]{:S(2)}, u32[]{:S(2)}) async-start(bf16[8,4,63,512]{3,1,2,0:T(4,128)(2,1)} %copy.17), calls=%async_computation.2 | async-start | bytes 4128768 | tf_op jit(solution)/shard_map/all_to_all | solution.py:57
  142.8 7.0 %all-to-all-start.1 = ((s32[4,1,504]{2,1,0:T(1,128)}), s32[4,1,504]{2,1,0:T(1,128)S(1)}, u32[]{:S(2)}, u32[]{:S(2)}) async-start(s32[4,1,504]{2,1,0:T(1,128)} %reshape.287), calls=%async_computation.1 | async-start | bytes 16384 | tf_op jit(solution)/shard_map/all_to_all | solution.py:63
  149.8 29.8 %all-to-all-start.3 = ((bf16[8,4,63,512]{3,0,2,1:T(8,128)(2,1)}), bf16[8,4,63,512]{3,0,2,1:T(8,128)(2,1)}, u32[]{:S(2)}, u32[]{:S(2)}) async-start(bf16[8,4,63,512]{3,0,2,1:T(8,128)(2,1)} %copy.18), calls=%async_computation.3 | async-start | bytes 4128768 | tf_op jit(solution)/shard_map/all_to_all | solution.py:56
  183.5 16.2 %copy-start.2 = (s32[1024]{0:T(1024)S(1)}, s32[1024]{0:T(1024)}, u32[]{:S(2)}) copy-start(s32[1024]{0:T(1024)} %param.19) | copy-start | bytes 12292
  194.7 5.1 %collective-permute-start.1 = (bf16[2,256,512]{2,1,0:T(8,128)(2,1)S(1)}, bf16[2,256,512]{2,1,0:T(8,128)(2,1)S(1)}, u32[]{:S(2)}, u32[]{:S(2)}) collective-permute-start(bf16[2,256,512]{2,1,0:T(8,128)(2,1)S(1)} %bitcast.72), channel_id=1, source_target_pairs={{1,0},{2,1},{3,2},{4,3},{5,4},{6,5},{7,6},{8,7},{9,8},{10,9},{11,1... | collective-permute-start | bytes 1572872 | tf_op jit(solution)/shard_map/ppermute | solution.py:23
  196.0 4.6 %collective-permute-start = (bf16[2,256,512]{2,1,0:T(8,128)(2,1)S(1)}, bf16[2,256,512]{2,1,0:T(8,128)(2,1)S(1)}, u32[]{:S(2)}, u32[]{:S(2)}) collective-permute-start(bf16[2,256,512]{2,1,0:T(8,128)(2,1)S(1)} %bitcast.71), channel_id=1, source_target_pairs={{0,1},{1,2},{2,3},{3,4},{4,5},{5,6},{6,7},{7,8},{8,9},{9,10},{10,1... | collective-permute-start | bytes 1572872 | tf_op jit(solution)/shard_map/ppermute | solution.py:22
  268.0 16.0 %copy-start = (f32[8,256,512]{2,1,0:T(8,128)S(1)}, f32[8,256,512]{2,1,0:T(8,128)}, u32[]{:S(2)}) copy-start(f32[8,256,512]{2,1,0:T(8,128)} %get-tuple-element.150) | copy-start | bytes 12582916
  270.7 13.5 %collective-permute-start.2 = (bf16[2,256,512]{2,1,0:T(8,128)(2,1)S(1)}, bf16[2,256,512]{2,1,0:T(8,128)(2,1)S(1)}, u32[]{:S(2)}, u32[]{:S(2)}) collective-permute-start(bf16[2,256,512]{2,1,0:T(8,128)(2,1)S(1)} %get-tuple-element.217), channel_id=1, source_target_pairs={{0,1},{1,2},{2,3},{3,4},{4,5},{5,6},{6,7},{7,8},{8,9},{9,10},{10,1... | collective-permute-start | bytes 1572872 | tf_op jit(solution)/shard_map/ppermute | solution.py:31
  282.7 5.6 %collective-permute-start.3 = (bf16[2,256,512]{2,1,0:T(8,128)(2,1)S(1)}, bf16[2,256,512]{2,1,0:T(8,128)(2,1)S(1)}, u32[]{:S(2)}, u32[]{:S(2)}) collective-permute-start(bf16[2,256,512]{2,1,0:T(8,128)(2,1)S(1)} %get-tuple-element.216), channel_id=1, source_target_pairs={{1,0},{2,1},{3,2},{4,3},{5,4},{6,5},{7,6},{8,7},{9,8},{10,9},{11,1... | collective-permute-start | bytes 1572872 | tf_op jit(solution)/shard_map/ppermute | solution.py:31
where the time goes:
time: 400 us; the launch traced here: 398 us
  local copies, waits for them, and re-layouts  128 us (32%)
  blocking collectives  87.5 us (22%)
  waiting for transfers between devices  76 us (19%)
  other arithmetic  44.9 us (11%)
  starting transfers between devices  38.8 us (10%)
  matrix products  21 us (5%)
    all_to_all x1, blocking collectives, body(): lax.all_to_all(back_rows, 'mass', split_axis=0, concat_axis=0, tiled=True)  59.7 us
    gather x11, local copies, waits for them, and re-layouts, body(): group_start = jnp.searchsorted(sorted_owners, sorted_owners, side='left')  49.8 us
    all_to_all x1, waiting for transfers between devices, body(): lax.all_to_all(send_rows, 'mass', split_axis=0, concat_axis=0, tiled=True)  45 us
    scatter-add x4, other arithmetic, block_step(): ext_grad = ext_grad.at[chosen].add(tile_grad.reshape(NB, TILE_ROWS, width))  30.6 us
    all_to_all x1, blocking collectives, body(): lax.all_to_all(lax.all_to_all(back_rows, 'mass', split_axis=0, concat_axi...  27.8 us
    all_to_all x1, waiting for transfers between devices, body(): lax.all_to_all(lax.all_to_all(send_rows, 'mass', split_axis=0, concat_axi...  24.3 us
    ppermute x2, starting transfers between devices, shifted(): lax.ppermute(value, axis, [(source, source + steps) for source in range(l...  13.3 us
    scatter x1, local copies, waits for them, and re-layouts, body(): jnp.zeros((pep_rows + 1, width), jnp.bfloat16).at[target].set(got_rows)  11.1 us
  transfers between devices with their start and end apart: 8, of which 5 were waited for; matrix products, arithmetic and copies ran while one was open for 4% of the time, Pallas kernels for 0%

commit v1 on v0

v1 whole, which is shorter than its diff:
```python
import functools
import math

import jax
import jax.numpy as jnp
from jax import lax
from jax.experimental import pallas as pl
from jax.experimental.pallas import tpu as pltpu
from jax.sharding import PartitionSpec as P

TILE_ROWS = 256
EDGE = 2
NB = 6
TILE_DEV = 4
SB = 4
CHUNK = 256
AXES = ("mass", "prot")
BASE = 256


def log2(value):
    bits = value.bit_length() - 1
    assert value == 1 << bits
    return bits


def iota(shape, dim):
    return lax.broadcasted_iota(jnp.int32, shape, dim)


def onehot(mask):
    return jnp.where(mask, 1.0, 0.0).astype(jnp.bfloat16)


def matmul(a, b, dims=((1,), (0,))):
    return lax.dot_general(a, b, (dims, ((), ())), preferred_element_type=jnp.float32)


def pack_kernel(devices, block, dest_ref, pep_ref, send_ref, pos_ref, meta_ref):
    step = pl.program_id(0)
    rows = pep_ref.shape[0]
    width = pep_ref.shape[1]

    @pl.when(step == 0)
    def _():
        dest = dest_ref[...]
        owner = lax.shift_right_logical(dest, log2(rows))
        filled = dest - owner * rows + 1
        member = iota((devices, rows), 0) == owner
        before = onehot(iota((rows, rows), 0) < iota((rows, rows), 1))
        seen = matmul(onehot(member), before)
        rank = jnp.sum(jnp.where(member, seen, 0.0), axis=0, keepdims=True).astype(jnp.int32)
        position = owner * block + rank
        for c in range(rows // CHUNK):
            pos_ref[c : c + 1, :] = position[:, c * CHUNK : (c + 1) * CHUNK]
        high = lax.shift_right_logical(filled, log2(BASE))
        low = filled - high * BASE
        lane = iota((2 * CHUNK, rows), 0)
        part = jnp.where(lane < CHUNK, high.astype(jnp.float32), low.astype(jnp.float32))
        spread = jnp.where((lane & (block - 1)) == rank, part, 0.0).astype(jnp.bfloat16)
        meta_ref[...] = matmul(onehot(member), spread, ((1,), (1,))).astype(jnp.bfloat16)

    base = step * CHUNK
    position = jnp.concatenate([pos_ref[c : c + 1, :] for c in range(rows // CHUNK)], axis=1)
    pick = onehot(iota((CHUNK, rows), 0) + base == position)
    place = onehot(
        iota((CHUNK, devices), 0) + base == iota((CHUNK, devices), 1) * block + (block - 1)
    )
    sent = matmul(pick, pep_ref[...])
    extra = matmul(place, meta_ref[...])
    send_ref[...] = (sent + extra).astype(jnp.bfloat16)


def pack(destination, peptides, devices, block):
    rows, width = peptides.shape
    slots = devices * block
    assert width == 2 * CHUNK and CHUNK % block == 0 and slots % CHUNK == 0
    return pl.pallas_call(
        functools.partial(pack_kernel, devices, block),
        grid=(slots // CHUNK,),
        in_specs=[
            pl.BlockSpec((1, rows), lambda c: (0, 0)),
            pl.BlockSpec((rows, width), lambda c: (0, 0)),
        ],
        out_specs=[
            pl.BlockSpec((CHUNK, width), lambda c: (c, 0)),
            pl.BlockSpec((rows // CHUNK, CHUNK), lambda c: (0, 0)),
        ],
        out_shape=[
            jax.ShapeDtypeStruct((slots, width), jnp.bfloat16),
            jax.ShapeDtypeStruct((rows // CHUNK, CHUNK), jnp.int32),
        ],
        scratch_shapes=[pltpu.VMEM((devices, width), jnp.bfloat16)],
        name="pack",
    )(destination.reshape(1, rows), peptides)


def unpack_kernel(block, got_ref, table_ref, slot_ref, pick_ref):
    step = pl.program_id(0)
    chunks = got_ref.shape[0] // CHUNK

    @pl.when(step == 0)
    def _():
        lane = iota((CHUNK, CHUNK), 1)
        tail = iota((CHUNK, CHUNK), 0) == lane - (lane & (block - 1)) + (block - 1)
        for q in range(chunks):
            part = got_ref[q * CHUNK : (q + 1) * CHUNK, :].astype(jnp.float32)
            high = jnp.sum(jnp.where(tail, part[:, :CHUNK], 0.0), axis=0, keepdims=True)
            low = jnp.sum(jnp.where(tail, part[:, CHUNK:], 0.0), axis=0, keepdims=True)
            slot_ref[q : q + 1, :] = (high * BASE + low).astype(jnp.int32) - 1

    row = iota((CHUNK, CHUNK), 0) + step * CHUNK
    for q in range(chunks):
        pick_ref[:, q * CHUNK : (q + 1) * CHUNK] = onehot(row == slot_ref[q : q + 1, :])
    table_ref[...] = matmul(pick_ref[...], got_ref[...]).astype(jnp.bfloat16)


def unpack(got, rows, block):
    slots, width = got.shape
    return pl.pallas_call(
        functools.partial(unpack_kernel, block),
        grid=(rows // CHUNK,),
        in_specs=[pl.BlockSpec((slots, width), lambda c: (0, 0))],
        out_specs=[
            pl.BlockSpec((CHUNK, width), lambda c: (c, 0)),
            pl.BlockSpec((slots // CHUNK, CHUNK), lambda c: (0, 0)),
        ],
        out_shape=[
            jax.ShapeDtypeStruct((rows, width), jnp.bfloat16),
            jax.ShapeDtypeStruct((slots // CHUNK, CHUNK), jnp.int32),
        ],
        scratch_shapes=[pltpu.VMEM((CHUNK, slots), jnp.bfloat16)],
        name="unpack",
    )(got)


def main_kernel(
    band_ref,
    factor_ref,
    before_ref,
    own_ref,
    after_ref,
    spec_ref,
    pos_ref,
    spec_grad_ref,
    left_ref,
    mine_ref,
    right_ref,
    ext_ref,
    grad_ref,
    sems,
):
    k = pl.program_id(0)
    edge = EDGE * TILE_ROWS
    mine = TILE_DEV * TILE_ROWS
    scaling = factor_ref[0]
    offset = factor_ref[1]

    @pl.when(k == 0)
    def _():
        copies = [
            pltpu.make_async_copy(before_ref, ext_ref.at[pl.ds(0, edge)], sems.at[0]),
            pltpu.make_async_copy(own_ref, ext_ref.at[pl.ds(edge, mine)], sems.at[1]),
            pltpu.make_async_copy(after_ref, ext_ref.at[pl.ds(edge + mine, edge)], sems.at[2]),
        ]
        for copy in copies:
            copy.start()
        grad_ref[...] = jnp.zeros_like(grad_ref)
        for copy in copies:
            copy.wait()

    spec = spec_ref[...]
    wanted = pos_ref[0]
    row = iota((TILE_ROWS, TILE_ROWS), 0)
    total = jnp.zeros(spec.shape, jnp.float32)
    for j in range(NB):
        start = pl.multiple_of(band_ref[k * NB + j] * TILE_ROWS, TILE_ROWS)
        tile = ext_ref[pl.ds(start, TILE_ROWS), :]
        logits = scaling * matmul(tile, spec, ((1,), (1,))) + offset
        labels = jnp.where(row + j * TILE_ROWS == wanted, 1.0, 0.0)
        weights = (jax.nn.sigmoid(logits) - labels).astype(jnp.bfloat16)
        grad_ref[pl.ds(start, TILE_ROWS), :] += matmul(weights, spec)
        total += matmul(weights, tile, ((0,), (0,)))
    spec_grad_ref[...] = (scaling * total).astype(jnp.bfloat16)

    @pl.when(k == SB - 1)
    def _():
        left_ref[...] = (scaling * grad_ref[:edge, :]).astype(jnp.bfloat16)
        mine_ref[...] = scaling * grad_ref[edge : edge + mine, :]
        right_ref[...] = (scaling * grad_ref[edge + mine :, :]).astype(jnp.bfloat16)


def gradients(band, factors, before, own, after, spectra, positive):
    width = spectra.shape[1]
    edge = EDGE * TILE_ROWS
    mine = TILE_DEV * TILE_ROWS
    anywhere = pl.BlockSpec(memory_space=pl.ANY)
    whole = lambda r: pl.BlockSpec((r, width), lambda k, *_: (0, 0))
    return pl.pallas_call(
        main_kernel,
        grid_spec=pltpu.PrefetchScalarGridSpec(
            num_scalar_prefetch=2,
            grid=(SB,),
            in_specs=[
                anywhere,
                anywhere,
                anywhere,
                pl.BlockSpec((TILE_ROWS, width), lambda k, *_: (k, 0)),
                pl.BlockSpec((1, 1, TILE_ROWS), lambda k, *_: (k, 0, 0)),
            ],
            out_specs=[
                pl.BlockSpec((TILE_ROWS, width), lambda k, *_: (k, 0)),
                whole(edge),
                whole(mine),
                whole(edge),
            ],
            scratch_shapes=[
                pltpu.VMEM((2 * edge + mine, width), jnp.bfloat16),
                pltpu.VMEM((2 * edge + mine, width), jnp.float32),
                pltpu.SemaphoreType.DMA((3,)),
            ],
        ),
        out_shape=[
            jax.ShapeDtypeStruct((SB * TILE_ROWS, width), jnp.bfloat16),
            jax.ShapeDtypeStruct((edge, width), jnp.bfloat16),
            jax.ShapeDtypeStruct((mine, width), jnp.float32),
            jax.ShapeDtypeStruct((edge, width), jnp.bfloat16),
        ],
        name="gradients",
    )(band, factors, before, own, after, spectra, positive)


def columns_of(row):
    tall = jnp.broadcast_to(row.astype(jnp.float32), (128, row.shape[1]))
    return jnp.transpose(tall).astype(jnp.int32)


def back_kernel(slot_ref, mine_ref, left_ref, right_ref, back_ref, grad_ref, pick_ref):
    step = pl.program_id(0)
    rows = mine_ref.shape[0]
    edge = left_ref.shape[0]

    @pl.when(step == 0)
    def _():
        lower = mine_ref[:edge, :] + left_ref[...].astype(jnp.float32)
        grad_ref[:edge, :] = lower.astype(jnp.bfloat16)
        upper = mine_ref[rows - edge :, :] + right_ref[...].astype(jnp.float32)
        grad_ref[rows - edge :, :] = upper.astype(jnp.bfloat16)

    slot = columns_of(slot_ref[pl.ds(step, 1), :])
    lane = iota(slot.shape, 1)
    for m in range(rows // 128):
        pick_ref[:, m * 128 : (m + 1) * 128] = onehot(lane + m * 128 == slot)
    back_ref[...] = matmul(pick_ref[...], grad_ref[...]).astype(jnp.bfloat16)


def send_back(slot, mine, from_left, from_right):
    rows, width = mine.shape
    edge = from_left.shape[0]
    assert rows == 2 * edge
    chunks = slot.shape[0]
    return pl.pallas_call(
        back_kernel,
        grid=(chunks,),
        in_specs=[
            pl.BlockSpec((chunks, CHUNK), lambda c: (0, 0)),
            pl.BlockSpec((rows, width), lambda c: (0, 0)),
            pl.BlockSpec((edge, width), lambda c: (0, 0)),
            pl.BlockSpec((edge, width), lambda c: (0, 0)),
        ],
        out_specs=pl.BlockSpec((CHUNK, width), lambda c: (c, 0)),
        out_shape=jax.ShapeDtypeStruct((chunks * CHUNK, width), jnp.bfloat16),
        scratch_shapes=[
            pltpu.VMEM((rows, width), jnp.bfloat16),
            pltpu.VMEM((CHUNK, rows), jnp.bfloat16),
        ],
        name="send_back",
    )(slot, mine, from_left, from_right)


def home_kernel(pos_ref, got_ref, out_ref, pick_ref):
    step = pl.program_id(0)
    position = columns_of(pos_ref[pl.ds(step, 1), :])
    lane = iota(position.shape, 1)
    for m in range(got_ref.shape[0] // 128):
        pick_ref[:, m * 128 : (m + 1) * 128] = onehot(lane + m * 128 == position)
    out_ref[...] = matmul(pick_ref[...], got_ref[...]).astype(jnp.bfloat16)


def home(position, returned):
    slots, width = returned.shape
    chunks = position.shape[0]
    return pl.pallas_call(
        home_kernel,
        grid=(chunks,),
        in_specs=[
            pl.BlockSpec((chunks, CHUNK), lambda c: (0, 0)),
            pl.BlockSpec((slots, width), lambda c: (0, 0)),
        ],
        out_specs=pl.BlockSpec((CHUNK, width), lambda c: (c, 0)),
        out_shape=jax.ShapeDtypeStruct((chunks * CHUNK, width), jnp.bfloat16),
        scratch_shapes=[pltpu.VMEM((CHUNK, slots), jnp.bfloat16)],
        name="home",
    )(position, returned)


def shifted(value, steps):
    count = lax.axis_size("mass") * lax.axis_size("prot")
    first, last = (max(0, -steps), min(count, count - steps))
    return lax.ppermute(value, AXES, [(source, source + steps) for source in range(first, last)])


def body(spectra, peptides, destination, band, positive, logit_scale, logit_bias):
    devices = lax.axis_size("mass") * lax.axis_size("prot")
    rows, width = peptides.shape
    edge = EDGE * TILE_ROWS
    block = 2 * (rows // devices)
    factors = jnp.concatenate([logit_scale / math.sqrt(width), logit_bias])

    send, position = pack(destination, peptides, devices, block)
    got = lax.all_to_all(send, AXES, 0, 0, tiled=True)
    table, slot = unpack(got, rows, block)
    before = shifted(table[rows - edge :], 1)
    after = shifted(table[:edge], -1)
    spec_grad, to_left, mine, to_right = gradients(
        band.reshape(-1), factors, before, table, after, spectra,
        positive.reshape(SB, 1, TILE_ROWS),
    )
    from_right = shifted(to_left, -1)
    from_left = shifted(to_right, 1)
    back = send_back(slot, mine, from_left, from_right)
    returned = lax.all_to_all(back, AXES, 0, 0, tiled=True)
    return (spec_grad, home(position, returned))


def solution(mesh):
    in_specs = (
        P(AXES, None),
        P(AXES, None),
        P(AXES),
        P(AXES, None),
        P(AXES),
        P(),
        P(),
    )
    out_specs = (P(AXES, None), P(AXES, None))
    return jax.shard_map(body, mesh=mesh, in_specs=in_specs, out_specs=out_specs, check_vma=False)
```

time: 400 us -> 186 us (0.47)
  local copies, waits for them, and re-layouts: 128 us -> 3.73 us
  waiting for transfers between devices: 76 us -> 4.67 us
  other arithmetic: 44.9 us -> 0.65 us
  Pallas kernels: 0 us -> 41 us
  blocking collectives: 87.5 us -> 116 us
  starting transfers between devices: 38.8 us -> 17.1 us
  matrix products: 21 us -> 0 us
    gather x18 -> x0, local copies, waits for them, and re-layouts: 77.5 us -> none  [the longest x11 49.8 us: body(): group_start = jnp.searchsorted(sorted_owners, sorted_owners, side='left')]
    all_to_all x4 -> x0, waiting for transfers between devices: 71.4 us -> none  [the longest x1 45 us: body(): lax.all_to_all(send_rows, 'mass', split_axis=0, concat_axis=0, tiled=True)]
    pallas_call x0 -> x5, Pallas kernels: none -> 41 us  [the longest x1 15.2 us: gradients(): pl.pallas_call(main_kernel, grid_spec=pltpu.PrefetchScalarGridSpec(num_sc...]
    scatter-add x6 -> x0, other arithmetic: 31.1 us -> none  [the longest x4 30.6 us: block_step(): ext_grad = ext_grad.at[chosen].add(tile_grad.reshape(NB, TILE_ROWS, width))]
    all_to_all x2, blocking collectives: 87.5 us -> 116 us  [the longest x1 60.1 us: body(): returned = lax.all_to_all(back, AXES, 0, 0, tiled=True)]
    scatter x4 -> x0, local copies, waits for them, and re-layouts: 26.8 us -> none  [the longest x1 11.1 us: body(): jnp.zeros((pep_rows + 1, width), jnp.bfloat16).at[target].set(got_rows)]
    all_to_all x4 -> x0, starting transfers between devices: 21.2 us -> none  [the longest x1 7.31 us: body(): lax.all_to_all(send_slots, 'mass', split_axis=0, concat_axis=0, tiled=True)]
    dot_general x12 -> x0, matrix products: 21 us -> none  [the longest x4 9.59 us: block_step(): jnp.einsum('rd,cd->rc', spec_block, columns, preferred_element_type=jnp.f...]
  transfers between devices with their start and end apart: 8 -> 4, of which waited for: 5 -> 2; matrix products, arithmetic and copies ran while one was open for 4% -> 1% of each run, Pallas kernels for 0% -> 0%
where the time goes in v1:
time: 186 us; the launch traced here: 185 us
  blocking collectives  116 us (62%)
  Pallas kernels  41 us (22%)
  starting transfers between devices  17.1 us (9%)
  waiting for transfers between devices  4.67 us (3%)
  local copies, waits for them, and re-layouts  3.73 us (2%)
  between operations  2 us (1%)
    all_to_all x1, blocking collectives, body(): returned = lax.all_to_all(back, AXES, 0, 0, tiled=True)  60.1 us
    all_to_all x1, blocking collectives, body(): got = lax.all_to_all(send, AXES, 0, 0, tiled=True)  56.1 us
    ppermute x4, starting transfers between devices, shifted(): lax.ppermute(value, AXES, [(source, source + steps) for source in range(f...  17.1 us
    pallas_call x1, Pallas kernels, gradients(): pl.pallas_call(main_kernel, grid_spec=pltpu.PrefetchScalarGridSpec(num_sc...  15.2 us
    pallas_call x1, Pallas kernels, send_back(): pl.pallas_call(back_kernel, grid=(chunks,), in_specs=[pl.BlockSpec((chunk...  7.7 us
    pallas_call x1, Pallas kernels, pack(): pl.pallas_call(functools.partial(pack_kernel, devices, block), grid=(slot...  7.19 us
    pallas_call x1, Pallas kernels, unpack(): pl.pallas_call(functools.partial(unpack_kernel, block), grid=(rows // CHU...  5.49 us
    pallas_call x1, Pallas kernels, home(): pl.pallas_call(home_kernel, grid=(chunks,), in_specs=[pl.BlockSpec((chunk...  5.47 us
  transfers between devices with their start and end apart: 4, of which 2 were waited for; matrix products, arithmetic and copies ran while one was open for 1% of the time, Pallas kernels for 0%

profile of v1, /device:TPU:0, one launch (start us, length us, event | category | flops | bytes accessed | tf_op | source)
XLA Modules:
  0.0 185.4 jit_solution(4148967855010204072)
XLA Ops:
  0.6 7.2 %pack.1 = (bf16[2048,512]{1,0:T(8,128)(2,1)}, s32[4,256]{1,0:T(4,128)}) custom-call(s32[1,1024]{1,0:T(1,128)} %bitcast.10, bf16[1024,512]{1,0:T(8,128)(2,1)} %pep_ref.1), custom_call_target="tpu_custom_call" | custom-call | tf_op jit(solution)/shard_map/pack/pallas_call | solution.py:78
  7.8 56.1 %all_to_all.22 = bf16[32,64,512]{2,1,0:T(8,128)(2,1)} all-to-all(bf16[32,64,512]{2,1,0:T(8,128)(2,1)} %bitcast.9), channel_id=1, replica_groups=mesh['mass'=8,'prot'=4] {'mass','prot'}, dimensions={0} | all-to-all | bytes 4194304 | tf_op jit(solution)/shard_map/all_to_all | solution.py:321
  63.9 0.0 copy-start.4
  63.9 5.5 %unpack.1 = (bf16[1024,512]{1,0:T(8,128)(2,1)}, s32[8,256]{1,0:T(8,128)}) custom-call(bf16[2048,512]{1,0:T(8,128)(2,1)} %bitcast.7), custom_call_target="tpu_custom_call" | custom-call | tf_op jit(solution)/shard_map/unpack/pallas_call | solution.py:120
  69.4 1.3 fusion
  70.7 1.3 collective-permute-start.1
  72.0 3.1 %collective-permute-start = (bf16[512,512]{1,0:T(8,128)(2,1)S(1)}, bf16[512,512]{1,0:T(8,128)(2,1)S(1)}, u32[]{:S(2)}, u32[]{:S(2)}) collective-permute-start(bf16[512,512]{1,0:T(8,128)(2,1)S(1)} %get-tuple-element.19), channel_id=1, source_target_pairs={{0,1},{1,2},{2,3},{3,4},{4,5},{5,6},{6,7},{7,8},{8,9},{9,10},{10,1... | collective-permute-start | bytes 1572872 | tf_op jit(solution)/shard_map/ppermute | solution.py:310
  76.4 0.0 copy-done.4
  76.4 0.7 reshape.17.band_ref
  77.1 0.7 pad_maximum_fusion.factor_ref
  77.7 0.0 collective-permute-done.1.after_ref
  77.7 0.0 copy-start.2
  77.7 0.0 collective-permute-done.before_ref
  77.7 0.0 copy-start.3
  77.7 0.8 copy-done.2
  78.5 0.2 copy-done.3
  78.7 15.2 %gradients.1 = (bf16[1024,512]{1,0:T(8,128)(2,1)}, bf16[512,512]{1,0:T(8,128)(2,1)}, f32[1024,512]{1,0:T(8,128)}, bf16[512,512]{1,0:T(8,128)(2,1)}) custom-call(s32[24]{0:T(128)} %reshape.17.band_ref, f32[2]{0:T(128)} %pad_maximum_fusion.factor_ref, bf16[512,512]{1,0:T(8,128)(2,1)} %copy-done.3, bf16[1024,512]{1,0:T(8,128)(2,1)} %get-tuple-element.11.own_ref, ...), custom_call_target="tpu_custom_call" | custom-call | tf_op jit(solution)/shard_map/gradients/pallas_call | solution.py:199
  93.9 11.4 %collective-permute-start.2 = (bf16[512,512]{1,0:T(8,128)(2,1)}, bf16[512,512]{1,0:T(8,128)(2,1)S(1)}, u32[]{:S(2)}, u32[]{:S(2)}) collective-permute-start(bf16[512,512]{1,0:T(8,128)(2,1)} %get-tuple-element.16), channel_id=1, source_target_pairs={{0,1},{1,2},{2,3},{3,4},{4,5},{5,6},{6,7},{7,8},{8,9},{9,10},{10,1... | collective-permute-start | bytes 1572872 | tf_op jit(solution)/shard_map/ppermute | solution.py:310
  105.3 1.3 collective-permute-start.3
  106.6 0.4 collective-permute-done.2.left_ref
  107.0 0.0 copy-start
  107.0 4.3 %collective-permute-done.3.right_ref = bf16[512,512]{1,0:T(8,128)(2,1)S(1)} collective-permute-done((bf16[512,512]{1,0:T(8,128)(2,1)}, bf16[512,512]{1,0:T(8,128)(2,1)S(1)}, u32[]{:S(2)}, u32[]{:S(2)}) %collective-permute-start.3) | collective-permute-done | bytes 524320 | tf_op jit(solution)/shard_map/ppermute | solution.py:310
  111.3 0.0 copy-start.1
  111.3 0.0 copy-done
  111.3 0.8 copy-done.1
  112.1 7.7 %send_back.1 = bf16[2048,512]{1,0:T(8,128)(2,1)} custom-call(s32[8,256]{1,0:T(8,128)} %get-tuple-element.14.slot_ref, f32[1024,512]{1,0:T(8,128)} %get-tuple-element.15.mine_ref, bf16[512,512]{1,0:T(8,128)(2,1)} %copy-done, bf16[512,512]{1,0:T(8,128)(2,1)} %copy-done.1), custom_call_target="tpu_custom_call" | custom-call | tf_op jit(solution)/shard_map/send_back/pallas_call | solution.py:262
  119.8 60.1 %all_to_all.23 = bf16[32,64,512]{2,1,0:T(8,128)(2,1)} all-to-all(bf16[32,64,512]{2,1,0:T(8,128)(2,1)} %bitcast.6), channel_id=1, replica_groups=mesh['mass'=8,'prot'=4] {'mass','prot'}, dimensions={0} | all-to-all | bytes 4194304 | tf_op jit(solution)/shard_map/all_to_all | solution.py:332
  179.9 5.5 %home.1 = bf16[1024,512]{1,0:T(8,128)(2,1)} custom-call(s32[4,256]{1,0:T(4,128)} %get-tuple-element.13.pos_ref, bf16[2048,512]{1,0:T(8,128)(2,1)} %bitcast.8), custom_call_target="tpu_custom_call" | custom-call | tf_op jit(solution)/shard_map/home/pallas_call | solution.py:293
Async XLA Ops:
  63.9 12.4 %copy-start.4 = (s32[4,6]{1,0:T(4,128)S(1)}, s32[4,6]{1,0:T(4,128)}, u32[]{:S(2)}) copy-start(s32[4,6]{1,0:T(4,128)} %param.10) | copy-start | bytes 292
  70.7 7.0 %collective-permute-start.1 = (bf16[512,512]{1,0:T(8,128)(2,1)S(1)}, bf16[512,512]{1,0:T(8,128)(2,1)S(1)}, u32[]{:S(2)}, u32[]{:S(2)}) collective-permute-start(bf16[512,512]{1,0:T(8,128)(2,1)S(1)} %get-tuple-element.18), channel_id=1, source_target_pairs={{1,0},{2,1},{3,2},{4,3},{5,4},{6,5},{7,6},{8,7},{9,8},{10,9},{11,1... | collective-permute-start | bytes 1572872 | tf_op jit(solution)/shard_map/ppermute | solution.py:310
  72.0 5.7 %collective-permute-start = (bf16[512,512]{1,0:T(8,128)(2,1)S(1)}, bf16[512,512]{1,0:T(8,128)(2,1)S(1)}, u32[]{:S(2)}, u32[]{:S(2)}) collective-permute-start(bf16[512,512]{1,0:T(8,128)(2,1)S(1)} %get-tuple-element.19), channel_id=1, source_target_pairs={{0,1},{1,2},{2,3},{3,4},{4,5},{5,6},{6,7},{7,8},{8,9},{9,10},{10,1... | collective-permute-start | bytes 1572872 | tf_op jit(solution)/shard_map/ppermute | solution.py:310
  77.7 0.8 copy-start.2
  77.7 1.0 copy-start.3
  93.9 13.1 %collective-permute-start.2 = (bf16[512,512]{1,0:T(8,128)(2,1)}, bf16[512,512]{1,0:T(8,128)(2,1)S(1)}, u32[]{:S(2)}, u32[]{:S(2)}) collective-permute-start(bf16[512,512]{1,0:T(8,128)(2,1)} %get-tuple-element.16), channel_id=1, source_target_pairs={{0,1},{1,2},{2,3},{3,4},{4,5},{5,6},{6,7},{7,8},{8,9},{9,10},{10,1... | collective-permute-start | bytes 1572872 | tf_op jit(solution)/shard_map/ppermute | solution.py:310
  105.3 6.0 %collective-permute-start.3 = (bf16[512,512]{1,0:T(8,128)(2,1)}, bf16[512,512]{1,0:T(8,128)(2,1)S(1)}, u32[]{:S(2)}, u32[]{:S(2)}) collective-permute-start(bf16[512,512]{1,0:T(8,128)(2,1)} %get-tuple-element.17), channel_id=1, source_target_pairs={{1,0},{2,1},{3,2},{4,3},{5,4},{6,5},{7,6},{8,7},{9,8},{10,9},{11,1... | collective-permute-start | bytes 1572872 | tf_op jit(solution)/shard_map/ppermute | solution.py:310
  107.0 4.3 %copy-start = (bf16[512,512]{1,0:T(8,128)(2,1)}, bf16[512,512]{1,0:T(8,128)(2,1)S(1)}, u32[]{:S(2)}) copy-start(bf16[512,512]{1,0:T(8,128)(2,1)S(1)} %collective-permute-done.2.left_ref) | copy-start | bytes 1572868
  111.3 0.8 copy-start.1

commit v2 on v0

v2 whole, which is shorter than its diff:
```python
import functools
import math

import jax
import jax.numpy as jnp
from jax import lax
from jax.experimental import pallas as pl
from jax.experimental.pallas import tpu as pltpu
from jax.sharding import PartitionSpec as P


TILE_ROWS = 256
EDGE = 2
NB = 6
TILE_DEV = 4
SB = 4
CHUNK = 256
AXES = ("mass", "prot")
BASE = 256
GROUP = 2
WIDE = GROUP * CHUNK
VMEM_LIMIT = 24 * 1024 * 1024
PARAMS = pltpu.CompilerParams(vmem_limit_bytes=VMEM_LIMIT)
IN_VMEM = pl.BlockSpec(memory_space=pltpu.VMEM)
IN_SMEM = pl.BlockSpec(memory_space=pltpu.SMEM)
ANYWHERE = pl.BlockSpec(memory_space=pl.ANY)
IN_HBM = pl.BlockSpec(memory_space=pltpu.HBM)


def log2(value):
    bits = value.bit_length() - 1
    assert value == 1 << bits
    return bits


def iota(shape, dim):
    return lax.broadcasted_iota(jnp.int32, shape, dim)


def onehot(mask):
    return jnp.where(mask, 1.0, 0.0).astype(jnp.bfloat16)


def matmul(a, b, dims=((1,), (0,))):
    return lax.dot_general(a, b, (dims, ((), ())), preferred_element_type=jnp.float32)


def chunk_copy(source, target, sems, c):
    part = pl.ds(pl.multiple_of(c * WIDE, WIDE), WIDE)
    return pltpu.make_async_copy(source.at[part], target.at[part], sems.at[c])


def in_hbm(value):
    return pltpu.with_memory_space_constraint(value, pltpu.HBM)


def pack_kernel(
    devices,
    block,
    dest_any,
    pep_any,
    want_any,
    band_any,
    send_ref,
    pos_ref,
    info_ref,
    dest_ref,
    pep_ref,
    want_ref,
    band_ref,
    meta_ref,
    rows_ref,
    load_sems,
    sems,
):
    rows = pep_ref.shape[0]
    pairs = [(dest_any, dest_ref), (want_any, want_ref), (band_any, band_ref), (pep_any, pep_ref)]
    loads = [pltpu.make_async_copy(*pair, load_sems.at[n]) for n, pair in enumerate(pairs)]
    for load in loads:
        load.start()
    for load in loads[:3]:
        load.wait()
    info_ref[...] = jnp.zeros_like(info_ref)
    for k in range(SB):
        info_ref[k : k + 1, :] = want_ref[k]
    info_ref[SB:, :NB] = band_ref[...] + 1

    dest = dest_ref[...]
    owner = lax.shift_right_logical(dest, log2(rows))
    filled = dest - owner * rows + 1
    member = iota((devices, rows), 0) == owner
    before = onehot(iota((rows, rows), 0) < iota((rows, rows), 1))
    seen = matmul(onehot(member), before)
    rank = jnp.sum(jnp.where(member, seen, 0.0), axis=0, keepdims=True).astype(jnp.int32)
    position = owner * block + rank
    for c in range(rows // CHUNK):
        pos_ref[c : c + 1, :] = position[:, c * CHUNK : (c + 1) * CHUNK]
    high = lax.shift_right_logical(filled, log2(BASE))
    low = filled - high * BASE
    lane = iota((2 * CHUNK, rows), 0)
    part = jnp.where(lane < CHUNK, high.astype(jnp.float32), low.astype(jnp.float32))
    spread = jnp.where((lane & (block - 1)) == rank, part, 0.0).astype(jnp.bfloat16)
    meta_ref[...] = matmul(onehot(member), spread, ((1,), (1,))).astype(jnp.bfloat16)

    loads[3].wait()

    def chunk(c, carry):
        base = c * WIDE
        place = jnp.concatenate([pos_ref[q : q + 1, :] for q in range(rows // CHUNK)], axis=1)
        pick = onehot(iota((WIDE, rows), 0) + base == place)
        tail = onehot(
            iota((WIDE, devices), 0) + base == iota((WIDE, devices), 1) * block + (block - 1)
        )
        sent = matmul(pick, pep_ref[...]) + matmul(tail, meta_ref[...])
        rows_ref[pl.ds(pl.multiple_of(base, WIDE), WIDE), :] = sent.astype(jnp.bfloat16)
        chunk_copy(rows_ref, send_ref, sems, c).start()
        return carry

    lax.fori_loop(0, send_ref.shape[0] // WIDE, chunk, 0)
    for c in range(send_ref.shape[0] // WIDE):
        chunk_copy(rows_ref, send_ref, sems, c).wait()


def pack(destination, peptides, positive, band, devices, block):
    rows, width = peptides.shape
    slots = devices * block
    operands = (
        destination.reshape(1, rows), peptides, positive.reshape(SB, 1, TILE_ROWS), band
    )
    assert width == 2 * CHUNK and CHUNK % block == 0 and slots % WIDE == 0
    return pl.pallas_call(
        functools.partial(pack_kernel, devices, block),
        in_specs=[IN_HBM] * 4,
        out_specs=[IN_HBM, IN_VMEM, IN_VMEM],
        out_shape=[
            pltpu.HBM((slots, width), jnp.bfloat16),
            jax.ShapeDtypeStruct((rows // CHUNK, CHUNK), jnp.int32),
            jax.ShapeDtypeStruct((2 * SB, TILE_ROWS), jnp.int32),
        ],
        scratch_shapes=[
            pltpu.VMEM((1, rows), jnp.int32),
            pltpu.VMEM((rows, width), jnp.bfloat16),
            pltpu.VMEM((SB, 1, TILE_ROWS), jnp.int32),
            pltpu.VMEM((SB, NB), jnp.int32),
            pltpu.VMEM((devices, width), jnp.bfloat16),
            pltpu.VMEM((slots, width), jnp.bfloat16),
            pltpu.SemaphoreType.DMA((4,)),
            pltpu.SemaphoreType.DMA((slots // WIDE,)),
        ],
        compiler_params=PARAMS,
        name="pack",
    )(*map(in_hbm, operands))


def columns_of(row):
    tall = jnp.broadcast_to(row.astype(jnp.float32), (128, row.shape[1]))
    return jnp.transpose(tall).astype(jnp.int32)


def weights_of(logits, half_scale, half_offset, wanted, shift):
    hit = iota(logits.shape, 0) + shift == wanted
    base = jnp.where(hit, -0.5, 0.5)
    return (0.5 * jnp.tanh(logits * half_scale + half_offset) + base).astype(jnp.bfloat16)


def unpack_kernel(
    block,
    got_ref,
    spec_prev,
    spec_own,
    spec_next,
    table_ref,
    slot_ref,
    spec_ref,
    low_ref,
    high_ref,
    pick_ref,
    spec_sems,
    sems,
):
    chunks = got_ref.shape[0] // CHUNK
    dev_rows = SB * TILE_ROWS
    loads = [
        pltpu.make_async_copy(spec, spec_ref.at[pl.ds(n * dev_rows, dev_rows)], spec_sems.at[n])
        for n, spec in enumerate((spec_prev, spec_own, spec_next))
    ]
    for load in loads:
        load.start()

    lane = iota((CHUNK, CHUNK), 1)
    tail = iota((CHUNK, CHUNK), 0) == lane - (lane & (block - 1)) + (block - 1)
    for q in range(chunks):
        part = got_ref[q * CHUNK : (q + 1) * CHUNK, :].astype(jnp.float32)
        high = jnp.sum(jnp.where(tail, part[:, :CHUNK], 0.0), axis=0, keepdims=True)
        low = jnp.sum(jnp.where(tail, part[:, CHUNK:], 0.0), axis=0, keepdims=True)
        slot_ref[q : q + 1, :] = (high * BASE + low).astype(jnp.int32) - 1

    stores = []
    for half, edge_ref in enumerate((low_ref, high_ref)):

        edge = EDGE * TILE_ROWS
        row = iota((edge, CHUNK), 0) + half * edge
        for q in range(chunks):
            pick_ref[:, q * CHUNK : (q + 1) * CHUNK] = onehot(row == slot_ref[q : q + 1, :])
        half_table = matmul(pick_ref[...], got_ref[...]).astype(jnp.bfloat16)
        table_ref[half * edge : (half + 1) * edge, :] = half_table
        store = pltpu.make_async_copy(
            table_ref.at[pl.ds(half * edge, edge)], edge_ref, sems.at[half]
        )
        store.start()
        stores.append(store)
    for copy in stores + loads:
        copy.wait()


def unpack(got, spectra, block):
    slots, width = got.shape
    rows = TILE_DEV * TILE_ROWS
    chunks = slots // CHUNK
    assert TILE_DEV == 2 * EDGE and CHUNK == TILE_ROWS
    half = pltpu.HBM((rows // 2, width), jnp.bfloat16)
    return pl.pallas_call(
        functools.partial(unpack_kernel, block),
        in_specs=[IN_VMEM] + [ANYWHERE] * 3,
        out_specs=[IN_VMEM] * 3 + [IN_HBM] * 2,
        out_shape=[
            jax.ShapeDtypeStruct((rows, width), jnp.bfloat16),
            jax.ShapeDtypeStruct((chunks, CHUNK), jnp.int32),
            jax.ShapeDtypeStruct((3 * SB * TILE_ROWS, width), jnp.bfloat16),
            half,
            half,
        ],
        scratch_shapes=[
            pltpu.VMEM((EDGE * TILE_ROWS, slots), jnp.bfloat16),
            pltpu.SemaphoreType.DMA((3,)),
            pltpu.SemaphoreType.DMA((2,)),
        ],
        compiler_params=PARAMS,
        name="unpack",
    )(got, *map(in_hbm, spectra))


def tiles_kernel(
    scale_ref,
    bias_ref,
    table_ref,
    slot_ref,
    spec_ref,
    info_prev,
    info_own,
    info_next,
    band_prev,
    band_own,
    band_next,
    back_ref,
    mask_ref,
    weight_ref,
    grad_ref,
    rows_ref,
    sems,
):
    chunks = slot_ref.shape[0]
    rows = grad_ref.shape[0]
    dev_rows = SB * TILE_ROWS
    scaling = scale_ref[0] * (1.0 / math.sqrt(table_ref.shape[1]))
    infos = (info_prev, info_own, info_next)
    bands = (band_prev, band_own, band_next)

    edge = EDGE * TILE_ROWS
    for upper in range(TILE_DEV // EDGE):
        pair = table_ref[upper * edge : (upper + 1) * edge, :]
        for source in (upper, upper + 1):
            for k in range(SB):
                first = (source * SB + k) * TILE_ROWS
                column = first - upper * dev_rows
                logits = matmul(pair, spec_ref[first : first + TILE_ROWS, :], ((1,), (1,)))
                for e in range(EDGE):
                    tag = upper * EDGE + e + (EDGE + TILE_DEV * (1 - source) + 1)
                    place = jnp.int32(-1)
                    for j in range(NB):
                        place = jnp.where(bands[source][SB + k, j] == tag, j, place)
                    active = place >= 0
                    span = slice(e * TILE_ROWS, (e + 1) * TILE_ROWS)
                    weight_ref[span, column : column + TILE_ROWS] = weights_of(
                        logits[span, :],
                        jnp.where(active, 0.5 * scaling, 0.0),
                        jnp.where(active, 0.5 * bias_ref[0], -1e30),
                        infos[source][k : k + 1, :],
                        jnp.where(active, place, 2 * NB) * TILE_ROWS,
                    )
        total = matmul(weight_ref[...], spec_ref[upper * dev_rows : (upper + 2) * dev_rows, :])
        grad_ref[upper * edge : (upper + 1) * edge, :] = (scaling * total).astype(jnp.bfloat16)

    def back_step(q, carry):
        for g in range(GROUP):
            slot = columns_of(slot_ref[pl.ds(q * GROUP + g, 1), :])
            lane = iota(slot.shape, 1)
            for m in range(rows // 128):
                mask_ref[g * CHUNK : (g + 1) * CHUNK, m * 128 : (m + 1) * 128] = onehot(
                    lane + m * 128 == slot
                )
        start = pl.multiple_of(q * WIDE, WIDE)
        rows_ref[pl.ds(start, WIDE), :] = matmul(mask_ref[...], grad_ref[...]).astype(jnp.bfloat16)
        chunk_copy(rows_ref, back_ref, sems, q).start()
        return carry

    lax.fori_loop(0, chunks // GROUP, back_step, 0)
    for q in range(chunks // GROUP):
        chunk_copy(rows_ref, back_ref, sems, q).wait()


def tiles(scale, bias, table, slot, spectra, infos):
    rows, width = table.shape
    chunks = slot.shape[0]
    slots = chunks * CHUNK
    return pl.pallas_call(
        tiles_kernel,
        in_specs=[IN_SMEM] * 2 + [IN_VMEM] * 6 + [IN_SMEM] * 3,
        out_specs=IN_HBM,
        out_shape=pltpu.HBM((slots, width), jnp.bfloat16),
        scratch_shapes=[
            pltpu.VMEM((WIDE, rows), jnp.bfloat16),
            pltpu.VMEM((EDGE * TILE_ROWS, 2 * SB * TILE_ROWS), jnp.bfloat16),
            pltpu.VMEM((rows, width), jnp.bfloat16),
            pltpu.VMEM((slots, width), jnp.bfloat16),
            pltpu.SemaphoreType.DMA((chunks,)),
        ],
        compiler_params=PARAMS,
        name="tiles",
    )(scale, bias, table, slot, spectra, *infos, *infos)


def spectra_kernel(
    scale_ref, bias_ref, band_ref, before_ref, own_ref, after_ref, spec_ref, info_ref,
    out_ref, ext_ref, sems,
):
    k = pl.program_id(0)
    edge = EDGE * TILE_ROWS
    scaling = scale_ref[0] * (1.0 / math.sqrt(out_ref.shape[1]))

    @pl.when(k == 0)
    def _():
        mine = TILE_DEV * TILE_ROWS
        copies = [
            pltpu.make_async_copy(before_ref, ext_ref.at[pl.ds(0, edge)], sems.at[0]),
            pltpu.make_async_copy(own_ref, ext_ref.at[pl.ds(edge, mine)], sems.at[1]),
            pltpu.make_async_copy(after_ref, ext_ref.at[pl.ds(edge + mine, edge)], sems.at[2]),
        ]
        for copy in copies:
            copy.start()
        for copy in copies:
            copy.wait()

    total = jnp.zeros(out_ref.shape, jnp.float32)
    for j in range(NB):
        start = pl.multiple_of((band_ref[SB + k, j] - 1) * TILE_ROWS, TILE_ROWS)
        tile = ext_ref[pl.ds(start, TILE_ROWS), :]
        weights = weights_of(
            matmul(tile, spec_ref[...], ((1,), (1,))),
            0.5 * scaling,
            0.5 * bias_ref[0],
            info_ref[pl.ds(k, 1), :],
            j * TILE_ROWS,
        )
        total += matmul(weights, tile, ((0,), (0,)))
    out_ref[...] = (scaling * total).astype(jnp.bfloat16)


def spectra_gradient(scale, bias, info, before, table, after, spectra):
    width = spectra.shape[1]
    edge = EDGE * TILE_ROWS
    return pl.pallas_call(
        spectra_kernel,
        grid=(SB,),
        in_specs=[
            IN_SMEM,
            IN_SMEM,
            IN_SMEM,
            ANYWHERE,
            ANYWHERE,
            ANYWHERE,
            pl.BlockSpec((TILE_ROWS, width), lambda k: (k, 0)),
            pl.BlockSpec((2 * SB, TILE_ROWS), lambda k: (0, 0)),
        ],
        out_specs=pl.BlockSpec((TILE_ROWS, width), lambda k: (k, 0)),
        scratch_shapes=[
            pltpu.VMEM((4 * edge, width), jnp.bfloat16),
            pltpu.SemaphoreType.DMA((3,)),
        ],
        compiler_params=PARAMS,
        out_shape=jax.ShapeDtypeStruct((SB * TILE_ROWS, width), jnp.bfloat16),
        name="spectra_gradient",
    )(scale, bias, info, before, table, after, spectra, info)


def home_kernel(pos_ref, got_ref, out_ref, pick_ref, grad_ref, sems):
    chunks = pos_ref.shape[0]

    def chunk(c, carry):
        for g in range(GROUP):
            position = columns_of(pos_ref[pl.ds(c * GROUP + g, 1), :])
            lane = iota(position.shape, 1)
            for m in range(got_ref.shape[0] // 128):
                pick_ref[g * CHUNK : (g + 1) * CHUNK, m * 128 : (m + 1) * 128] = onehot(
                    lane + m * 128 == position
                )
        grad = matmul(pick_ref[...], got_ref[...]).astype(jnp.bfloat16)
        grad_ref[pl.ds(pl.multiple_of(c * WIDE, WIDE), WIDE), :] = grad
        chunk_copy(grad_ref, out_ref, sems, c).start()
        return carry

    lax.fori_loop(0, chunks // GROUP, chunk, 0)
    for c in range(chunks // GROUP):
        chunk_copy(grad_ref, out_ref, sems, c).wait()


def home(position, returned):
    slots, width = returned.shape
    chunks = position.shape[0]
    rows = chunks * CHUNK
    return pl.pallas_call(
        home_kernel,
        in_specs=[IN_VMEM] * 2,
        out_specs=IN_HBM,
        out_shape=jax.ShapeDtypeStruct((rows, width), jnp.bfloat16),
        scratch_shapes=[
            pltpu.VMEM((WIDE, slots), jnp.bfloat16),
            pltpu.VMEM((rows, width), jnp.bfloat16),
            pltpu.SemaphoreType.DMA((chunks,)),
        ],
        compiler_params=PARAMS,
        name="home",
    )(position, returned)


def shifted(value, steps):
    count = lax.axis_size("mass") * lax.axis_size("prot")
    first, last = (max(0, -steps), min(count, count - steps))
    return lax.ppermute(value, AXES, [(source, source + steps) for source in range(first, last)])


def program(spectra, peptides, destination, band, positive, logit_scale, logit_bias):
    devices = lax.axis_size("mass") * lax.axis_size("prot")
    rows = peptides.shape[0]
    block = 2 * (rows // devices)

    spec_prev = shifted(spectra, 1)
    spec_next = shifted(spectra, -1)
    send, position, info = pack(destination, peptides, positive, band, devices, block)
    info_prev = shifted(info, 1)
    info_next = shifted(info, -1)
    got = lax.all_to_all(send, AXES, 0, 0, tiled=True)
    table, slot, specs, low, high = unpack(got, (spec_prev, spectra, spec_next), block)
    after = shifted(low, -1)
    before = shifted(high, 1)
    back = tiles(logit_scale, logit_bias, table, slot, specs, (info_prev, info, info_next))
    returned = lax.all_to_all(back, AXES, 0, 0, tiled=True)
    spec_grad = spectra_gradient(logit_scale, logit_bias, info, before, table, after, spectra)
    return (spec_grad, home(position, returned))


def solution(mesh):
    in_specs = (
        P(AXES, None),
        P(AXES, None),
        P(AXES),
        P(AXES, None),
        P(AXES),
        P(),
        P(),
    )
    out_specs = (P(AXES, None), P(AXES, None))
    return jax.shard_map(program, mesh=mesh, in_specs=in_specs, out_specs=out_specs, check_vma=False)
```

time: 400 us -> 161 us (0.40)
  the two profiles are of different devices: /device:TPU:0 before, /device:TPU:16 now
where the time goes in v2:
time: 161 us
  waiting for transfers between devices  91.3 us (57%)
  Pallas kernels  33.9 us (21%)
  starting transfers between devices  31.1 us (19%)
  local copies, waits for them, and re-layouts  2.21 us (1%)
  between operations  2.09 us (1%)
    ppermute x6, waiting for transfers between devices, shifted(): lax.ppermute(value, AXES, [(source, source + steps) for source in range(f...  91.3 us
    ppermute x6, starting transfers between devices, shifted(): lax.ppermute(value, AXES, [(source, source + steps) for source in range(f...  22.1 us
    pallas_call x1, Pallas kernels, tiles(): pl.pallas_call(tiles_kernel, in_specs=[IN_SMEM] * 2 + [IN_VMEM] * 6 + [IN...  10.5 us
    pallas_call x1, Pallas kernels, spectra_gradient(): pl.pallas_call(spectra_kernel, grid=(SB,), in_specs=[IN_SMEM, IN_SMEM, IN...  10.4 us
    all_to_all x1, starting transfers between devices, program(): got = lax.all_to_all(send, AXES, 0, 0, tiled=True)  5.95 us
    pallas_call x1, Pallas kernels, pack(): pl.pallas_call(functools.partial(pack_kernel, devices, block), in_specs=[...  5.55 us
    pallas_call x1, Pallas kernels, unpack(): pl.pallas_call(functools.partial(unpack_kernel, block), in_specs=[IN_VMEM...  3.73 us
    pallas_call x1, Pallas kernels, home(): pl.pallas_call(home_kernel, in_specs=[IN_VMEM] * 2, out_specs=IN_HBM, out...  3.68 us
  transfers between devices with their start and end apart: 8, of which 2 were waited for; matrix products, arithmetic and copies ran while one was open for 0% of the time, Pallas kernels for 9%

profile of v2, /device:TPU:16, one launch (start us, length us, event | category | flops | bytes accessed | tf_op | source)
XLA Modules:
  0.0 160.6 jit_solution(10028378891832935192)
XLA Ops:
  0.6 5.5 %pack.1 = (bf16[2048,512]{1,0:T(8,128)(2,1)}, s32[4,256]{1,0:T(4,128)S(1)}, s32[8,256]{1,0:T(8,128)S(1)}) custom-call(s32[1,1024]{1,0:T(1,128)} %bitcast.10, bf16[1024,512]{1,0:T(8,128)(2,1)} %pep_any.1, s32[4,1,256]{2,1,0:T(1,128)} %bitcast.11, s32[4,6]{1,0:T(4,128)} %band_any.1), custom_call_target="tpu_custom_call" | custom-call | tf_op jit(solution)/shard_map/pack/pallas_call | solution.py:131
  6.2 0.0 copy-start
  6.2 6.0 %all-to-all-start = ((bf16[32,64,512]{2,1,0:T(8,128)(2,1)}), bf16[32,64,512]{2,1,0:T(8,128)(2,1)S(1)}, u32[]{:S(2)}, u32[]{:S(2)}) async-start(bf16[32,64,512]{2,1,0:T(8,128)(2,1)} %bitcast.9), calls=%async_computation | async-start | bytes 4194304 | tf_op jit(solution)/shard_map/all_to_all | solution.py:452
  12.2 0.0 copy-done
  12.2 2.0 %collective-permute-start = (bf16[1024,512]{1,0:T(8,128)(2,1)S(1)}, bf16[1024,512]{1,0:T(8,128)(2,1)S(1)}, u32[]{:S(2)}, u32[]{:S(2)}) collective-permute-start(bf16[1024,512]{1,0:T(8,128)(2,1)S(1)} %copy-done), channel_id=1, source_target_pairs={{0,1},{1,2},{2,3},{3,4},{4,5},{5,6},{6,7},{7,8},{8,9},{9,10},{10,1... | collective-permute-start | bytes 3145736 | tf_op jit(solution)/shard_map/ppermute | solution.py:439
  14.2 5.3 %collective-permute-start.1 = (bf16[1024,512]{1,0:T(8,128)(2,1)S(1)}, bf16[1024,512]{1,0:T(8,128)(2,1)}, u32[]{:S(2)}, u32[]{:S(2)}) collective-permute-start(bf16[1024,512]{1,0:T(8,128)(2,1)S(1)} %copy-done), channel_id=1, source_target_pairs={{1,0},{2,1},{3,2},{4,3},{5,4},{6,5},{7,6},{8,7},{9,8},{10,9},{11,1... | collective-permute-start | bytes 3145736 | tf_op jit(solution)/shard_map/ppermute | solution.py:439
  19.5 1.9 %collective-permute-start.4 = (s32[8,256]{1,0:T(8,128)S(1)}, s32[8,256]{1,0:T(8,128)S(1)}, u32[]{:S(2)}, u32[]{:S(2)}) collective-permute-start(s32[8,256]{1,0:T(8,128)S(1)} %get-tuple-element.10.band_ref.info_ref.info_own.band_own), channel_id=1, source_target_pairs={{0,1},{1,2},{2,3},{3,4},{4,5},{5,6},{6,7},{7,8},{8,9},{9,10},{10,1... | collective-permute-start | bytes 24584 | tf_op jit(solution)/shard_map/ppermute | solution.py:439
  21.5 5.4 %collective-permute-start.5 = (s32[8,256]{1,0:T(8,128)S(1)}, s32[8,256]{1,0:T(8,128)S(1)}, u32[]{:S(2)}, u32[]{:S(2)}) collective-permute-start(s32[8,256]{1,0:T(8,128)S(1)} %get-tuple-element.10.band_ref.info_ref.info_own.band_own), channel_id=1, source_target_pairs={{1,0},{2,1},{3,2},{4,3},{5,4},{6,5},{7,6},{8,7},{9,8},{10,9},{11,1... | collective-permute-start | bytes 24584 | tf_op jit(solution)/shard_map/ppermute | solution.py:439
  28.2 44.2 %collective-permute-done.spec_prev = bf16[1024,512]{1,0:T(8,128)(2,1)S(1)} collective-permute-done((bf16[1024,512]{1,0:T(8,128)(2,1)S(1)}, bf16[1024,512]{1,0:T(8,128)(2,1)S(1)}, u32[]{:S(2)}, u32[]{:S(2)}) %collective-permute-start) | collective-permute-done | bytes 1048608 | tf_op jit(solution)/shard_map/ppermute | solution.py:439
  72.4 0.0 copy-start.4
  72.4 1.0 copy-done.4
  73.3 0.0 collective-permute-done.1.spec_next
  73.3 0.0 all-to-all-done
  73.3 3.7 %unpack.1 = (bf16[1024,512]{1,0:T(8,128)(2,1)S(1)}, s32[8,256]{1,0:T(8,128)S(1)}, bf16[3072,512]{1,0:T(8,128)(2,1)S(1)}, bf16[512,512]{1,0:T(8,128)(2,1)}, bf16[512,512]{1,0:T(8,128)(2,1)}) custom-call(bf16[2048,512]{1,0:T(8,128)(2,1)S(1)} %bitcast.6, bf16[1024,512]{1,0:T(8,128)(2,1)} %copy-done.4, bf16[1024,512]{1,0:T(8,128)(2,1)} %spec_ref.1, ...), custom_call_target="tpu_custom_call" | custom-call | tf_op jit(solution)/shard_map/unpack/pallas_call | solution.py:222
  77.1 0.0 copy-start.2
  77.1 0.0 collective-permute-done.4.info_prev.band_prev
  77.1 0.0 collective-permute-done.5.info_next.band_next
  77.1 10.5 %tiles.1 = bf16[2048,512]{1,0:T(8,128)(2,1)} custom-call(f32[1]{0:T(128)S(6)} %copy.9.scale_ref, f32[1]{0:T(128)S(6)} %copy.10.bias_ref, bf16[1024,512]{1,0:T(8,128)(2,1)S(1)} %get-tuple-element.13.own_ref.table_ref, s32[8,256]{1,0:T(8,128)S(1)} %get-tuple-element.16.slot_ref, bf16[3072,512]{1,0:T(8,128)(2,1)S(1)} %get-tuple-element.17.spec_ref, ...), custom_call_target="tpu_custom_call" | custom-call | tf_op jit(solution)/shard_map/tiles/pallas_call | solution.py:316
  87.6 0.0 copy-done.2
  87.7 0.0 copy-start.1
  87.7 3.0 %all-to-all-start.1 = ((bf16[32,64,512]{2,1,0:T(8,128)(2,1)}), bf16[32,64,512]{2,1,0:T(8,128)(2,1)S(1)}, u32[]{:S(2)}, u32[]{:S(2)}) async-start(bf16[32,64,512]{2,1,0:T(8,128)(2,1)} %bitcast.8), calls=%async_computation.1 | async-start | bytes 4194304 | tf_op jit(solution)/shard_map/all_to_all | solution.py:457
  90.7 2.0 %collective-permute-start.2 = (bf16[512,512]{1,0:T(8,128)(2,1)}, bf16[512,512]{1,0:T(8,128)(2,1)S(1)}, u32[]{:S(2)}, u32[]{:S(2)}) collective-permute-start(bf16[512,512]{1,0:T(8,128)(2,1)} %get-tuple-element.12), channel_id=1, source_target_pairs={{0,1},{1,2},{2,3},{3,4},{4,5},{5,6},{6,7},{7,8},{8,9},{9,10},{10,1... | collective-permute-start | bytes 1572872 | tf_op jit(solution)/shard_map/ppermute | solution.py:439
  92.7 5.3 %collective-permute-start.3 = (bf16[512,512]{1,0:T(8,128)(2,1)}, bf16[512,512]{1,0:T(8,128)(2,1)S(1)}, u32[]{:S(2)}, u32[]{:S(2)}) collective-permute-start(bf16[512,512]{1,0:T(8,128)(2,1)} %get-tuple-element.14), channel_id=1, source_target_pairs={{1,0},{2,1},{3,2},{4,3},{5,4},{6,5},{7,6},{8,7},{9,8},{10,9},{11,1... | collective-permute-start | bytes 1572872 | tf_op jit(solution)/shard_map/ppermute | solution.py:439
  98.1 47.1 %collective-permute-done.2.before_ref = bf16[512,512]{1,0:T(8,128)(2,1)S(1)} collective-permute-done((bf16[512,512]{1,0:T(8,128)(2,1)}, bf16[512,512]{1,0:T(8,128)(2,1)S(1)}, u32[]{:S(2)}, u32[]{:S(2)}) %collective-permute-start.2) | collective-permute-done | bytes 524320 | tf_op jit(solution)/shard_map/ppermute | solution.py:439
  145.2 0.0 collective-permute-done.3.after_ref
  145.2 0.0 copy-done.1
  145.2 0.0 copy-start.3
  145.2 1.2 copy-done.3
  146.5 10.4 %spectra_gradient.1 = bf16[1024,512]{1,0:T(8,128)(2,1)} custom-call(f32[1]{0:T(128)S(6)} %copy.9.scale_ref, f32[1]{0:T(128)S(6)} %copy.10.bias_ref, s32[8,256]{1,0:T(8,128)S(1)} %get-tuple-element.10.band_ref.info_ref.info_own.band_own, bf16[512,512]{1,0:T(8,128)(2,1)S(1)} %collective-permute-done.2.before_ref, bf16[1024,512]{1,0:T(8,128)(2,1)S(1)} %copy-done.3, ...), custom_call_target="tpu_custom_call" | custom-call | tf_op jit(solution)/shard_map/spectra_gradient/pallas_call | solution.py:372
  156.9 0.0 all-to-all-done.1
  156.9 3.7 %home.1 = bf16[1024,512]{1,0:T(8,128)(2,1)} custom-call(s32[4,256]{1,0:T(4,128)S(1)} %get-tuple-element.15.pos_ref, bf16[2048,512]{1,0:T(8,128)(2,1)S(1)} %bitcast.7), custom_call_target="tpu_custom_call" | custom-call | tf_op jit(solution)/shard_map/home/pallas_call | solution.py:421
Async XLA Ops:
  6.2 6.0 %copy-start = (bf16[1024,512]{1,0:T(8,128)(2,1)S(1)}, bf16[1024,512]{1,0:T(8,128)(2,1)}, u32[]{:S(2)}) copy-start(bf16[1024,512]{1,0:T(8,128)(2,1)} %spec_ref.1) | copy-start | bytes 3145732
  6.2 67.1 %all-to-all-start = ((bf16[32,64,512]{2,1,0:T(8,128)(2,1)}), bf16[32,64,512]{2,1,0:T(8,128)(2,1)S(1)}, u32[]{:S(2)}, u32[]{:S(2)}) async-start(bf16[32,64,512]{2,1,0:T(8,128)(2,1)} %bitcast.9), calls=%async_computation | async-start | bytes 4194304 | tf_op jit(solution)/shard_map/all_to_all | solution.py:452
  12.2 60.2 %collective-permute-start = (bf16[1024,512]{1,0:T(8,128)(2,1)S(1)}, bf16[1024,512]{1,0:T(8,128)(2,1)S(1)}, u32[]{:S(2)}, u32[]{:S(2)}) collective-permute-start(bf16[1024,512]{1,0:T(8,128)(2,1)S(1)} %copy-done), channel_id=1, source_target_pairs={{0,1},{1,2},{2,3},{3,4},{4,5},{5,6},{6,7},{7,8},{8,9},{9,10},{10,1... | collective-permute-start | bytes 3145736 | tf_op jit(solution)/shard_map/ppermute | solution.py:439
  14.2 59.1 %collective-permute-start.1 = (bf16[1024,512]{1,0:T(8,128)(2,1)S(1)}, bf16[1024,512]{1,0:T(8,128)(2,1)}, u32[]{:S(2)}, u32[]{:S(2)}) collective-permute-start(bf16[1024,512]{1,0:T(8,128)(2,1)S(1)} %copy-done), channel_id=1, source_target_pairs={{1,0},{2,1},{3,2},{4,3},{5,4},{6,5},{7,6},{8,7},{9,8},{10,9},{11,1... | collective-permute-start | bytes 3145736 | tf_op jit(solution)/shard_map/ppermute | solution.py:439
  19.5 57.6 %collective-permute-start.4 = (s32[8,256]{1,0:T(8,128)S(1)}, s32[8,256]{1,0:T(8,128)S(1)}, u32[]{:S(2)}, u32[]{:S(2)}) collective-permute-start(s32[8,256]{1,0:T(8,128)S(1)} %get-tuple-element.10.band_ref.info_ref.info_own.band_own), channel_id=1, source_target_pairs={{0,1},{1,2},{2,3},{3,4},{4,5},{5,6},{6,7},{7,8},{8,9},{9,10},{10,1... | collective-permute-start | bytes 24584 | tf_op jit(solution)/shard_map/ppermute | solution.py:439
  21.5 55.6 %collective-permute-start.5 = (s32[8,256]{1,0:T(8,128)S(1)}, s32[8,256]{1,0:T(8,128)S(1)}, u32[]{:S(2)}, u32[]{:S(2)}) collective-permute-start(s32[8,256]{1,0:T(8,128)S(1)} %get-tuple-element.10.band_ref.info_ref.info_own.band_own), channel_id=1, source_target_pairs={{1,0},{2,1},{3,2},{4,3},{5,4},{6,5},{7,6},{8,7},{9,8},{10,9},{11,1... | collective-permute-start | bytes 24584 | tf_op jit(solution)/shard_map/ppermute | solution.py:439
  72.4 1.0 copy-start.4
  77.1 10.6 %copy-start.2 = (bf16[1024,512]{1,0:T(8,128)(2,1)}, bf16[1024,512]{1,0:T(8,128)(2,1)S(1)}, u32[]{:S(2)}) copy-start(bf16[1024,512]{1,0:T(8,128)(2,1)S(1)} %get-tuple-element.13.own_ref.table_ref) | copy-start | bytes 3145732
  87.7 57.6 %copy-start.1 = (bf16[1024,512]{1,0:T(8,128)(2,1)S(1)}, bf16[1024,512]{1,0:T(8,128)(2,1)}, u32[]{:S(2)}) copy-start(bf16[1024,512]{1,0:T(8,128)(2,1)} %spec_ref.1) | copy-start | bytes 3145732
  87.7 69.2 %all-to-all-start.1 = ((bf16[32,64,512]{2,1,0:T(8,128)(2,1)}), bf16[32,64,512]{2,1,0:T(8,128)(2,1)S(1)}, u32[]{:S(2)}, u32[]{:S(2)}) async-start(bf16[32,64,512]{2,1,0:T(8,128)(2,1)} %bitcast.8), calls=%async_computation.1 | async-start | bytes 4194304 | tf_op jit(solution)/shard_map/all_to_all | solution.py:457
  90.7 54.5 %collective-permute-start.2 = (bf16[512,512]{1,0:T(8,128)(2,1)}, bf16[512,512]{1,0:T(8,128)(2,1)S(1)}, u32[]{:S(2)}, u32[]{:S(2)}) collective-permute-start(bf16[512,512]{1,0:T(8,128)(2,1)} %get-tuple-element.12), channel_id=1, source_target_pairs={{0,1},{1,2},{2,3},{3,4},{4,5},{5,6},{6,7},{7,8},{8,9},{9,10},{10,1... | collective-permute-start | bytes 1572872 | tf_op jit(solution)/shard_map/ppermute | solution.py:439
  92.7 52.5 %collective-permute-start.3 = (bf16[512,512]{1,0:T(8,128)(2,1)}, bf16[512,512]{1,0:T(8,128)(2,1)S(1)}, u32[]{:S(2)}, u32[]{:S(2)}) collective-permute-start(bf16[512,512]{1,0:T(8,128)(2,1)} %get-tuple-element.14), channel_id=1, source_target_pairs={{1,0},{2,1},{3,2},{4,3},{5,4},{6,5},{7,6},{8,7},{9,8},{10,9},{11,1... | collective-permute-start | bytes 1572872 | tf_op jit(solution)/shard_map/ppermute | solution.py:439
  145.2 1.2 copy-start.3

commit v3 on v2

--- a/solution.py
+++ b/solution.py
@@ -19,6 +19,7 @@
 BASE = 256
 GROUP = 2
 WIDE = GROUP * CHUNK
+LANES = 128
 VMEM_LIMIT = 24 * 1024 * 1024
 PARAMS = pltpu.CompilerParams(vmem_limit_bytes=VMEM_LIMIT)
 IN_VMEM = pl.BlockSpec(memory_space=pltpu.VMEM)
@@ -69,6 +70,8 @@
     want_ref,
     band_ref,
     meta_ref,
+    lower_ref,
+    upper_ref,
     rows_ref,
     load_sems,
     sems,
@@ -89,9 +92,17 @@
     owner = lax.shift_right_logical(dest, log2(rows))
     filled = dest - owner * rows + 1
     member = iota((devices, rows), 0) == owner
-    before = onehot(iota((rows, rows), 0) < iota((rows, rows), 1))
-    seen = matmul(onehot(member), before)
-    rank = jnp.sum(jnp.where(member, seen, 0.0), axis=0, keepdims=True).astype(jnp.int32)
+    groups = [
+        jnp.where(member[:, g : g + LANES], 1.0, 0.0) for g in range(0, rows, LANES)
+    ]
+    earlier = onehot(iota((LANES, LANES), 0) < iota((LANES, LANES), 1))
+    seen = []
+    count = jnp.zeros((devices, 1), jnp.float32)
+    for group in groups:
+        inside = matmul(group.astype(jnp.bfloat16), earlier) + count
+        seen.append(jnp.sum(group * inside, axis=0, keepdims=True))
+        count = count + jnp.sum(group, axis=1, keepdims=True)
+    rank = jnp.concatenate(seen, axis=1).astype(jnp.int32)
     position = owner * block + rank
     for c in range(rows // CHUNK):
         pos_ref[c : c + 1, :] = position[:, c * CHUNK : (c + 1) * CHUNK]
@@ -101,13 +112,15 @@
     part = jnp.where(lane < CHUNK, high.astype(jnp.float32), low.astype(jnp.float32))
     spread = jnp.where((lane & (block - 1)) == rank, part, 0.0).astype(jnp.bfloat16)
     meta_ref[...] = matmul(onehot(member), spread, ((1,), (1,))).astype(jnp.bfloat16)
-
+    lower_ref[...] = onehot(iota((CHUNK, rows), 0) == (position & (CHUNK - 1)))
+    upper_ref[...] = lax.shift_right_logical(position, log2(CHUNK))
     loads[3].wait()
 
     def chunk(c, carry):
         base = c * WIDE
-        place = jnp.concatenate([pos_ref[q : q + 1, :] for q in range(rows // CHUNK)], axis=1)
-        pick = onehot(iota((WIDE, rows), 0) + base == place)
+        pick = jnp.concatenate(
+            [lower_ref[...] * onehot(upper_ref[...] == c * GROUP + g) for g in range(GROUP)], axis=0
+        )
         tail = onehot(
             iota((WIDE, devices), 0) + base == iota((WIDE, devices), 1) * block + (block - 1)
         )
@@ -143,6 +156,8 @@
             pltpu.VMEM((SB, 1, TILE_ROWS), jnp.int32),
             pltpu.VMEM((SB, NB), jnp.int32),
             pltpu.VMEM((devices, width), jnp.bfloat16),
+            pltpu.VMEM((CHUNK, rows), jnp.bfloat16),
+            pltpu.VMEM((1, rows), jnp.int32),
             pltpu.VMEM((slots, width), jnp.bfloat16),
             pltpu.SemaphoreType.DMA((4,)),
             pltpu.SemaphoreType.DMA((slots // WIDE,)),
@@ -152,9 +167,16 @@
     )(*map(in_hbm, operands))
 
 
-def columns_of(row):
-    tall = jnp.broadcast_to(row.astype(jnp.float32), (128, row.shape[1]))
-    return jnp.transpose(tall).astype(jnp.int32)
+def columns_onehot(row, target_ref, first):
+    tall = jnp.broadcast_to(row.astype(jnp.float32), (LANES, row.shape[1]))
+    column = jnp.transpose(tall).astype(jnp.int32)
+    lower = onehot(iota(column.shape, 1) == (column & (LANES - 1)))
+    upper = lax.shift_right_arithmetic(column, log2(LANES)).astype(jnp.bfloat16)
+    zero = jnp.zeros_like(lower)
+    for m in range(target_ref.shape[1] // LANES):
+        target_ref[first : first + row.shape[1], m * LANES : (m + 1) * LANES] = jnp.where(
+            upper == jnp.bfloat16(m), lower, zero
+        )
 
 
 def weights_of(logits, half_scale, half_offset, wanted, shift):
@@ -165,55 +187,70 @@
 
 def unpack_kernel(
     block,
+    odd_ref,
     got_ref,
-    spec_prev,
+    spec_cross,
     spec_own,
-    spec_next,
+    spec_partner,
     table_ref,
     slot_ref,
     spec_ref,
-    low_ref,
-    high_ref,
-    pick_ref,
+    cross_ref,
+    partner_ref,
+    lower_ref,
     spec_sems,
     sems,
 ):
     chunks = got_ref.shape[0] // CHUNK
     dev_rows = SB * TILE_ROWS
+    odd = odd_ref[0]
+    slots = (2 * odd, 1, 2 - 2 * odd)
     loads = [
-        pltpu.make_async_copy(spec, spec_ref.at[pl.ds(n * dev_rows, dev_rows)], spec_sems.at[n])
-        for n, spec in enumerate((spec_prev, spec_own, spec_next))
+        pltpu.make_async_copy(
+            spec,
+            spec_ref.at[pl.ds(pl.multiple_of(slots[n] * dev_rows, dev_rows), dev_rows)],
+            spec_sems.at[n],
+        )
+        for n, spec in enumerate((spec_cross, spec_own, spec_partner))
     ]
     for load in loads:
         load.start()
 
     lane = iota((CHUNK, CHUNK), 1)
     tail = iota((CHUNK, CHUNK), 0) == lane - (lane & (block - 1)) + (block - 1)
+    uppers = []
     for q in range(chunks):
         part = got_ref[q * CHUNK : (q + 1) * CHUNK, :].astype(jnp.float32)
         high = jnp.sum(jnp.where(tail, part[:, :CHUNK], 0.0), axis=0, keepdims=True)
         low = jnp.sum(jnp.where(tail, part[:, CHUNK:], 0.0), axis=0, keepdims=True)
-        slot_ref[q : q + 1, :] = (high * BASE + low).astype(jnp.int32) - 1
-
-    stores = []
-    for half, edge_ref in enumerate((low_ref, high_ref)):
-
-        edge = EDGE * TILE_ROWS
-        row = iota((edge, CHUNK), 0) + half * edge
-        for q in range(chunks):
-            pick_ref[:, q * CHUNK : (q + 1) * CHUNK] = onehot(row == slot_ref[q : q + 1, :])
-        half_table = matmul(pick_ref[...], got_ref[...]).astype(jnp.bfloat16)
+        slot = (high * BASE + low).astype(jnp.int32) - 1
+        slot_ref[q : q + 1, :] = slot
+        span = slice(q * CHUNK, (q + 1) * CHUNK)
+        lower_ref[:, span] = onehot(iota((CHUNK, CHUNK), 0) == (slot & (CHUNK - 1)))
+        uppers.append(lax.shift_right_arithmetic(slot, log2(CHUNK)))
+    upper = jnp.concatenate(uppers, axis=1)
+
+    edge = EDGE * TILE_ROWS
+    for half in range(TILE_DEV // EDGE):
+        pick = jnp.concatenate(
+            [lower_ref[...] * onehot(upper == half * EDGE + e) for e in range(EDGE)], axis=0
+        )
+        half_table = matmul(pick, got_ref[...]).astype(jnp.bfloat16)
         table_ref[half * edge : (half + 1) * edge, :] = half_table
-        store = pltpu.make_async_copy(
-            table_ref.at[pl.ds(half * edge, edge)], edge_ref, sems.at[half]
-        )
+
+    here = pl.multiple_of(odd * edge, edge)
+    there = pl.multiple_of(edge - here, edge)
+    stores = [
+        pltpu.make_async_copy(table_ref.at[pl.ds(here, edge)], cross_ref, sems.at[0]),
+        pltpu.make_async_copy(table_ref.at[pl.ds(there, edge)], partner_ref, sems.at[1]),
+    ]
+    for store in stores:
         store.start()
-        stores.append(store)
     for copy in stores + loads:
         copy.wait()
 
 
-def unpack(got, spectra, block):
+def unpack(odd, got, spectra, block):
     slots, width = got.shape
     rows = TILE_DEV * TILE_ROWS
     chunks = slots // CHUNK
@@ -221,7 +258,7 @@
     half = pltpu.HBM((rows // 2, width), jnp.bfloat16)
     return pl.pallas_call(
         functools.partial(unpack_kernel, block),
-        in_specs=[IN_VMEM] + [ANYWHERE] * 3,
+        in_specs=[IN_SMEM, IN_VMEM] + [ANYWHERE] * 3,
         out_specs=[IN_VMEM] * 3 + [IN_HBM] * 2,
         out_shape=[
             jax.ShapeDtypeStruct((rows, width), jnp.bfloat16),
@@ -231,13 +268,13 @@
             half,
         ],
         scratch_shapes=[
-            pltpu.VMEM((EDGE * TILE_ROWS, slots), jnp.bfloat16),
+            pltpu.VMEM((CHUNK, slots), jnp.bfloat16),
             pltpu.SemaphoreType.DMA((3,)),
             pltpu.SemaphoreType.DMA((2,)),
         ],
         compiler_params=PARAMS,
         name="unpack",
-    )(got, *map(in_hbm, spectra))
+    )(odd, got, *map(in_hbm, spectra))
 
 
 def tiles_kernel(
@@ -260,7 +297,6 @@
     sems,
 ):
     chunks = slot_ref.shape[0]
-    rows = grad_ref.shape[0]
     dev_rows = SB * TILE_ROWS
     scaling = scale_ref[0] * (1.0 / math.sqrt(table_ref.shape[1]))
     infos = (info_prev, info_own, info_next)
@@ -293,12 +329,7 @@
 
     def back_step(q, carry):
         for g in range(GROUP):
-            slot = columns_of(slot_ref[pl.ds(q * GROUP + g, 1), :])
-            lane = iota(slot.shape, 1)
-            for m in range(rows // 128):
-                mask_ref[g * CHUNK : (g + 1) * CHUNK, m * 128 : (m + 1) * 128] = onehot(
-                    lane + m * 128 == slot
-                )
+            columns_onehot(slot_ref[pl.ds(q * GROUP + g, 1), :], mask_ref, g * CHUNK)
         start = pl.multiple_of(q * WIDE, WIDE)
         rows_ref[pl.ds(start, WIDE), :] = matmul(mask_ref[...], grad_ref[...]).astype(jnp.bfloat16)
         chunk_copy(rows_ref, back_ref, sems, q).start()
@@ -331,7 +362,7 @@
 
 
 def spectra_kernel(
-    scale_ref, bias_ref, band_ref, before_ref, own_ref, after_ref, spec_ref, info_ref,
+    scale_ref, bias_ref, odd_ref, band_ref, cross_ref, own_ref, partner_ref, spec_ref, info_ref,
     out_ref, ext_ref, sems,
 ):
     k = pl.program_id(0)
@@ -341,10 +372,12 @@
     @pl.when(k == 0)
     def _():
         mine = TILE_DEV * TILE_ROWS
+        low = pl.multiple_of(odd_ref[0] * (edge + mine), edge)
+        high = pl.multiple_of(edge + mine - low, edge)
         copies = [
-            pltpu.make_async_copy(before_ref, ext_ref.at[pl.ds(0, edge)], sems.at[0]),
+            pltpu.make_async_copy(cross_ref, ext_ref.at[pl.ds(low, edge)], sems.at[0]),
             pltpu.make_async_copy(own_ref, ext_ref.at[pl.ds(edge, mine)], sems.at[1]),
-            pltpu.make_async_copy(after_ref, ext_ref.at[pl.ds(edge + mine, edge)], sems.at[2]),
+            pltpu.make_async_copy(partner_ref, ext_ref.at[pl.ds(high, edge)], sems.at[2]),
         ]
         for copy in copies:
             copy.start()
@@ -366,7 +399,7 @@
     out_ref[...] = (scaling * total).astype(jnp.bfloat16)
 
 
-def spectra_gradient(scale, bias, info, before, table, after, spectra):
+def spectra_gradient(scale, bias, odd, info, cross, table, partner, spectra):
     width = spectra.shape[1]
     edge = EDGE * TILE_ROWS
     return pl.pallas_call(
@@ -376,6 +409,7 @@
             IN_SMEM,
             IN_SMEM,
             IN_SMEM,
+            IN_SMEM,
             ANYWHERE,
             ANYWHERE,
             ANYWHERE,
@@ -390,7 +424,7 @@
         compiler_params=PARAMS,
         out_shape=jax.ShapeDtypeStruct((SB * TILE_ROWS, width), jnp.bfloat16),
         name="spectra_gradient",
-    )(scale, bias, info, before, table, after, spectra, info)
+    )(scale, bias, odd, info, cross, table, partner, spectra, info)
 
 
 def home_kernel(pos_ref, got_ref, out_ref, pick_ref, grad_ref, sems):
@@ -398,12 +432,7 @@
 
     def chunk(c, carry):
         for g in range(GROUP):
-            position = columns_of(pos_ref[pl.ds(c * GROUP + g, 1), :])
-            lane = iota(position.shape, 1)
-            for m in range(got_ref.shape[0] // 128):
-                pick_ref[g * CHUNK : (g + 1) * CHUNK, m * 128 : (m + 1) * 128] = onehot(
-                    lane + m * 128 == position
-                )
+            columns_onehot(pos_ref[pl.ds(c * GROUP + g, 1), :], pick_ref, g * CHUNK)
         grad = matmul(pick_ref[...], got_ref[...]).astype(jnp.bfloat16)
         grad_ref[pl.ds(pl.multiple_of(c * WIDE, WIDE), WIDE), :] = grad
         chunk_copy(grad_ref, out_ref, sems, c).start()
@@ -433,10 +462,15 @@
     )(position, returned)
 
 
-def shifted(value, steps):
+def from_partner(value):
     count = lax.axis_size("mass") * lax.axis_size("prot")
-    first, last = (max(0, -steps), min(count, count - steps))
-    return lax.ppermute(value, AXES, [(source, source + steps) for source in range(first, last)])
+    return lax.ppermute(value, AXES, [(i, i ^ 1) for i in range(count)])
+
+
+def from_cross(value):
+    count = lax.axis_size("mass") * lax.axis_size("prot")
+    pairs = [(i, i + 1) for i in range(1, count - 1, 2)]
+    return lax.ppermute(value, AXES, pairs + [(j, i) for i, j in pairs])
 
 
 def program(spectra, peptides, destination, band, positive, logit_scale, logit_bias):
@@ -444,18 +478,26 @@
     rows = peptides.shape[0]
     block = 2 * (rows // devices)
 
-    spec_prev = shifted(spectra, 1)
-    spec_next = shifted(spectra, -1)
+    assert devices % 2 == 0
+    odd = (lax.axis_index(AXES) & 1).reshape(1)
+    spec_cross = from_cross(spectra)
+    spec_partner = from_partner(spectra)
     send, position, info = pack(destination, peptides, positive, band, devices, block)
-    info_prev = shifted(info, 1)
-    info_next = shifted(info, -1)
+    info_cross = from_cross(info)
+    info_partner = from_partner(info)
+    info_prev = jnp.where(odd == 1, info_partner, info_cross)
+    info_next = jnp.where(odd == 1, info_cross, info_partner)
     got = lax.all_to_all(send, AXES, 0, 0, tiled=True)
-    table, slot, specs, low, high = unpack(got, (spec_prev, spectra, spec_next), block)
-    after = shifted(low, -1)
-    before = shifted(high, 1)
+    table, slot, specs, to_cross, to_partner = unpack(
+        odd, got, (spec_cross, spectra, spec_partner), block
+    )
+    cross = from_cross(to_cross)
+    partner = from_partner(to_partner)
     back = tiles(logit_scale, logit_bias, table, slot, specs, (info_prev, info, info_next))
     returned = lax.all_to_all(back, AXES, 0, 0, tiled=True)
-    spec_grad = spectra_gradient(logit_scale, logit_bias, info, before, table, after, spectra)
+    spec_grad = spectra_gradient(
+        logit_scale, logit_bias, odd, info, cross, table, partner, spectra
+    )
     return (spec_grad, home(position, returned))
 
 

time: 161 us -> 160 us (level)
  waiting for transfers between devices: 91.3 us -> 102 us
  starting transfers between devices: 31.1 us -> 20.5 us
    ppermute x6, waiting for transfers between devices: 91.3 us -> 102 us  [the longest x3 102 us: from_cross(): return lax.ppermute(value, AXES, pairs + [(j, i) for i, j in pairs])]
    ppermute x6, starting transfers between devices: 22.1 us -> 11.6 us  [the longest x3 11.3 us: from_cross(): return lax.ppermute(value, AXES, pairs + [(j, i) for i, j in pairs])]
  transfers between devices with their start and end apart: 8 -> 8, of which waited for: 2 -> 2; matrix products, arithmetic and copies ran while one was open for 0% -> 0% of each run, Pallas kernels for 9% -> 7%
where the time goes in v3:
time: 160 us; the launch traced here: 159 us
  waiting for transfers between devices  102 us (64%)
  Pallas kernels  33.4 us (21%)
  starting transfers between devices  20.5 us (13%)
  between operations  2.1 us (1%)
    ppermute x3, waiting for transfers between devices, from_cross(): return lax.ppermute(value, AXES, pairs + [(j, i) for i, j in pairs])  102 us
    ppermute x3, starting transfers between devices, from_cross(): return lax.ppermute(value, AXES, pairs + [(j, i) for i, j in pairs])  11.3 us
    pallas_call x1, Pallas kernels, spectra_gradient(): pl.pallas_call(spectra_kernel, grid=(SB,), in_specs=[IN_SMEM, IN_SMEM, IN...  10.5 us
    pallas_call x1, Pallas kernels, tiles(): pl.pallas_call(tiles_kernel, in_specs=[IN_SMEM] * 2 + [IN_VMEM] * 6 + [IN...  10.1 us
    all_to_all x1, starting transfers between devices, program(): got = lax.all_to_all(send, AXES, 0, 0, tiled=True)  5.94 us
    pallas_call x1, Pallas kernels, pack(): pl.pallas_call(functools.partial(pack_kernel, devices, block), in_specs=[...  5.57 us
    pallas_call x1, Pallas kernels, unpack(): pl.pallas_call(functools.partial(unpack_kernel, block), in_specs=[IN_SMEM...  3.69 us
    pallas_call x1, Pallas kernels, home(): pl.pallas_call(home_kernel, in_specs=[IN_VMEM] * 2, out_specs=IN_HBM, out...  3.56 us
  transfers between devices with their start and end apart: 8, of which 2 were waited for; matrix products, arithmetic and copies ran while one was open for 0% of the time, Pallas kernels for 7%

profile of v3, /device:TPU:16, one launch (start us, length us, event | category | flops | bytes accessed | tf_op | source)
XLA Modules:
  0.0 159.2 jit_solution(3529316296507536557)
XLA Ops:
  0.6 5.6 %pack.1 = (bf16[2048,512]{1,0:T(8,128)(2,1)}, s32[4,256]{1,0:T(4,128)S(1)}, s32[8,256]{1,0:T(8,128)S(1)}) custom-call(s32[1,1024]{1,0:T(1,128)} %bitcast.12, bf16[1024,512]{1,0:T(8,128)(2,1)} %pep_any.1, s32[4,1,256]{2,1,0:T(1,128)} %bitcast.13, s32[4,6]{1,0:T(4,128)} %band_any.1), custom_call_target="tpu_custom_call" | custom-call | tf_op jit(solution)/shard_map/pack/pallas_call | solution.py:144
  6.2 0.0 copy-start
  6.2 5.9 %all-to-all-start = ((bf16[32,64,512]{2,1,0:T(8,128)(2,1)}), bf16[32,64,512]{2,1,0:T(8,128)(2,1)S(1)}, u32[]{:S(2)}, u32[]{:S(2)}) async-start(bf16[32,64,512]{2,1,0:T(8,128)(2,1)} %bitcast.11), calls=%async_computation | async-start | bytes 4194304 | tf_op jit(solution)/shard_map/all_to_all | solution.py:490
  12.2 0.0 copy-done
  12.2 4.0 %collective-permute-start = (bf16[1024,512]{1,0:T(8,128)(2,1)S(1)}, bf16[1024,512]{1,0:T(8,128)(2,1)}, u32[]{:S(2)}, u32[]{:S(2)}) collective-permute-start(bf16[1024,512]{1,0:T(8,128)(2,1)S(1)} %copy-done), channel_id=1, source_target_pairs={{1,2},{3,4},{5,6},{7,8},{9,10},{11,12},{13,14},{15,16},{17,18},{19... | collective-permute-start | bytes 3145736 | tf_op jit(solution)/shard_map/ppermute | solution.py:473
  16.2 0.1 collective-permute-start.1
  16.3 3.4 %collective-permute-start.5 = (s32[8,256]{1,0:T(8,128)S(1)}, s32[8,256]{1,0:T(8,128)S(1)}, u32[]{:S(2)}, u32[]{:S(2)}) collective-permute-start(s32[8,256]{1,0:T(8,128)S(1)} %get-tuple-element.10.band_ref.info_ref.info_own.band_own), channel_id=1, source_target_pairs={{1,2},{3,4},{5,6},{7,8},{9,10},{11,12},{13,14},{15,16},{17,18},{19... | collective-permute-start | bytes 24584 | tf_op jit(solution)/shard_map/ppermute | solution.py:473
  19.6 0.1 collective-permute-start.4
  21.0 51.5 %collective-permute-done.5 = s32[8,256]{1,0:T(8,128)S(1)} collective-permute-done((s32[8,256]{1,0:T(8,128)S(1)}, s32[8,256]{1,0:T(8,128)S(1)}, u32[]{:S(2)}, u32[]{:S(2)}) %collective-permute-start.5) | collective-permute-done | bytes 8224 | tf_op jit(solution)/shard_map/ppermute | solution.py:473
  72.5 0.0 collective-permute-done.4
  72.5 0.0 collective-permute-done.spec_cross
  72.5 0.0 collective-permute-done.1.spec_partner
  72.5 0.0 all-to-all-done
  72.5 3.7 %unpack.1 = (bf16[1024,512]{1,0:T(8,128)(2,1)S(1)}, s32[8,256]{1,0:T(8,128)S(1)}, bf16[3072,512]{1,0:T(8,128)(2,1)S(1)}, bf16[512,512]{1,0:T(8,128)(2,1)}, bf16[512,512]{1,0:T(8,128)(2,1)}) custom-call(s32[1]{0:T(128)} %bitcast.odd_ref, bf16[2048,512]{1,0:T(8,128)(2,1)S(1)} %bitcast.8, bf16[1024,512]{1,0:T(8,128)(2,1)} %collective-permute-done.spec_cross, ...), custom_call_target="tpu_custom_call" | custom-call | tf_op jit(solution)/shard_map/unpack/pallas_call | solution.py:259
  76.2 0.0 copy-start.2
  76.2 10.1 %tiles.1 = bf16[2048,512]{1,0:T(8,128)(2,1)} custom-call(f32[1]{0:T(128)S(6)} %copy.9.scale_ref, f32[1]{0:T(128)S(6)} %copy.10.bias_ref, bf16[1024,512]{1,0:T(8,128)(2,1)S(1)} %get-tuple-element.13.own_ref.table_ref, s32[8,256]{1,0:T(8,128)S(1)} %get-tuple-element.16.slot_ref, bf16[3072,512]{1,0:T(8,128)(2,1)S(1)} %get-tuple-element.17.spec_ref, ...), custom_call_target="tpu_custom_call" | custom-call | tf_op jit(solution)/shard_map/tiles/pallas_call | solution.py:347
  86.3 0.0 copy-done.2
  86.3 0.0 copy-start.1
  86.3 3.0 %all-to-all-start.1 = ((bf16[32,64,512]{2,1,0:T(8,128)(2,1)}), bf16[32,64,512]{2,1,0:T(8,128)(2,1)S(1)}, u32[]{:S(2)}, u32[]{:S(2)}) async-start(bf16[32,64,512]{2,1,0:T(8,128)(2,1)} %bitcast.10), calls=%async_computation.1 | async-start | bytes 4194304 | tf_op jit(solution)/shard_map/all_to_all | solution.py:497
  89.4 4.0 %collective-permute-start.2 = (bf16[512,512]{1,0:T(8,128)(2,1)}, bf16[512,512]{1,0:T(8,128)(2,1)S(1)}, u32[]{:S(2)}, u32[]{:S(2)}) collective-permute-start(bf16[512,512]{1,0:T(8,128)(2,1)} %get-tuple-element.12), channel_id=1, source_target_pairs={{1,2},{3,4},{5,6},{7,8},{9,10},{11,12},{13,14},{15,16},{17,18},{19... | collective-permute-start | bytes 1572872 | tf_op jit(solution)/shard_map/ppermute | solution.py:473
  93.4 0.1 collective-permute-start.3
  93.5 50.4 %collective-permute-done.2.cross_ref = bf16[512,512]{1,0:T(8,128)(2,1)S(1)} collective-permute-done((bf16[512,512]{1,0:T(8,128)(2,1)}, bf16[512,512]{1,0:T(8,128)(2,1)S(1)}, u32[]{:S(2)}, u32[]{:S(2)}) %collective-permute-start.2) | collective-permute-done | bytes 524320 | tf_op jit(solution)/shard_map/ppermute | solution.py:473
  143.9 0.0 collective-permute-done.3.partner_ref
  143.9 0.0 copy-done.1
  143.9 0.0 copy-start.3
  143.9 1.2 copy-done.3
  145.1 10.5 %spectra_gradient.1 = bf16[1024,512]{1,0:T(8,128)(2,1)} custom-call(f32[1]{0:T(128)S(6)} %copy.9.scale_ref, f32[1]{0:T(128)S(6)} %copy.10.bias_ref, s32[1]{0:T(128)} %bitcast.odd_ref, s32[8,256]{1,0:T(8,128)S(1)} %get-tuple-element.10.band_ref.info_ref.info_own.band_own, bf16[512,512]{1,0:T(8,128)(2,1)S(1)} %collective-permute-done.2.cross_ref, ...), custom_call_target="tpu_custom_call" | custom-call | tf_op jit(solution)/shard_map/spectra_gradient/pallas_call | solution.py:405
  155.6 0.0 all-to-all-done.1
  155.6 3.6 %home.1 = bf16[1024,512]{1,0:T(8,128)(2,1)} custom-call(s32[4,256]{1,0:T(4,128)S(1)} %get-tuple-element.15.pos_ref, bf16[2048,512]{1,0:T(8,128)(2,1)S(1)} %bitcast.9), custom_call_target="tpu_custom_call" | custom-call | tf_op jit(solution)/shard_map/home/pallas_call | solution.py:450
  (1 shorter events, 0.0 us)
Async XLA Ops:
  6.2 6.0 %copy-start = (bf16[1024,512]{1,0:T(8,128)(2,1)S(1)}, bf16[1024,512]{1,0:T(8,128)(2,1)}, u32[]{:S(2)}) copy-start(bf16[1024,512]{1,0:T(8,128)(2,1)} %spec_ref.1) | copy-start | bytes 3145732
  6.2 66.3 %all-to-all-start = ((bf16[32,64,512]{2,1,0:T(8,128)(2,1)}), bf16[32,64,512]{2,1,0:T(8,128)(2,1)S(1)}, u32[]{:S(2)}, u32[]{:S(2)}) async-start(bf16[32,64,512]{2,1,0:T(8,128)(2,1)} %bitcast.11), calls=%async_computation | async-start | bytes 4194304 | tf_op jit(solution)/shard_map/all_to_all | solution.py:490
  12.2 60.3 %collective-permute-start = (bf16[1024,512]{1,0:T(8,128)(2,1)S(1)}, bf16[1024,512]{1,0:T(8,128)(2,1)}, u32[]{:S(2)}, u32[]{:S(2)}) collective-permute-start(bf16[1024,512]{1,0:T(8,128)(2,1)S(1)} %copy-done), channel_id=1, source_target_pairs={{1,2},{3,4},{5,6},{7,8},{9,10},{11,12},{13,14},{15,16},{17,18},{19... | collective-permute-start | bytes 3145736 | tf_op jit(solution)/shard_map/ppermute | solution.py:473
  16.2 56.3 %collective-permute-start.1 = (bf16[1024,512]{1,0:T(8,128)(2,1)S(1)}, bf16[1024,512]{1,0:T(8,128)(2,1)}, u32[]{:S(2)}, u32[]{:S(2)}) collective-permute-start(bf16[1024,512]{1,0:T(8,128)(2,1)S(1)} %copy-done), channel_id=1, source_target_pairs={{0,1},{1,0},{2,3},{3,2},{4,5},{5,4},{6,7},{7,6},{8,9},{9,8},{10,11... | collective-permute-start | bytes 3145736 | tf_op jit(solution)/shard_map/ppermute | solution.py:467
  16.3 56.2 %collective-permute-start.5 = (s32[8,256]{1,0:T(8,128)S(1)}, s32[8,256]{1,0:T(8,128)S(1)}, u32[]{:S(2)}, u32[]{:S(2)}) collective-permute-start(s32[8,256]{1,0:T(8,128)S(1)} %get-tuple-element.10.band_ref.info_ref.info_own.band_own), channel_id=1, source_target_pairs={{1,2},{3,4},{5,6},{7,8},{9,10},{11,12},{13,14},{15,16},{17,18},{19... | collective-permute-start | bytes 24584 | tf_op jit(solution)/shard_map/ppermute | solution.py:473
  19.6 52.9 %collective-permute-start.4 = (s32[8,256]{1,0:T(8,128)S(1)}, s32[8,256]{1,0:T(8,128)S(1)}, u32[]{:S(2)}, u32[]{:S(2)}) collective-permute-start(s32[8,256]{1,0:T(8,128)S(1)} %get-tuple-element.10.band_ref.info_ref.info_own.band_own), channel_id=1, source_target_pairs={{0,1},{1,0},{2,3},{3,2},{4,5},{5,4},{6,7},{7,6},{8,9},{9,8},{10,11... | collective-permute-start | bytes 24584 | tf_op jit(solution)/shard_map/ppermute | solution.py:467
  76.2 10.1 %copy-start.2 = (bf16[1024,512]{1,0:T(8,128)(2,1)}, bf16[1024,512]{1,0:T(8,128)(2,1)S(1)}, u32[]{:S(2)}) copy-start(bf16[1024,512]{1,0:T(8,128)(2,1)S(1)} %get-tuple-element.13.own_ref.table_ref) | copy-start | bytes 3145732
  86.3 57.6 %copy-start.1 = (bf16[1024,512]{1,0:T(8,128)(2,1)S(1)}, bf16[1024,512]{1,0:T(8,128)(2,1)}, u32[]{:S(2)}) copy-start(bf16[1024,512]{1,0:T(8,128)(2,1)} %spec_ref.1) | copy-start | bytes 3145732
  86.3 69.3 %all-to-all-start.1 = ((bf16[32,64,512]{2,1,0:T(8,128)(2,1)}), bf16[32,64,512]{2,1,0:T(8,128)(2,1)S(1)}, u32[]{:S(2)}, u32[]{:S(2)}) async-start(bf16[32,64,512]{2,1,0:T(8,128)(2,1)} %bitcast.10), calls=%async_computation.1 | async-start | bytes 4194304 | tf_op jit(solution)/shard_map/all_to_all | solution.py:497
  89.4 54.5 %collective-permute-start.2 = (bf16[512,512]{1,0:T(8,128)(2,1)}, bf16[512,512]{1,0:T(8,128)(2,1)S(1)}, u32[]{:S(2)}, u32[]{:S(2)}) collective-permute-start(bf16[512,512]{1,0:T(8,128)(2,1)} %get-tuple-element.12), channel_id=1, source_target_pairs={{1,2},{3,4},{5,6},{7,8},{9,10},{11,12},{13,14},{15,16},{17,18},{19... | collective-permute-start | bytes 1572872 | tf_op jit(solution)/shard_map/ppermute | solution.py:473
  93.4 50.5 %collective-permute-start.3 = (bf16[512,512]{1,0:T(8,128)(2,1)}, bf16[512,512]{1,0:T(8,128)(2,1)S(1)}, u32[]{:S(2)}, u32[]{:S(2)}) collective-permute-start(bf16[512,512]{1,0:T(8,128)(2,1)} %get-tuple-element.14), channel_id=1, source_target_pairs={{0,1},{1,0},{2,3},{3,2},{4,5},{5,4},{6,7},{7,6},{8,9},{9,8},{10,11... | collective-permute-start | bytes 1572872 | tf_op jit(solution)/shard_map/ppermute | solution.py:467
  143.9 1.2 copy-start.3

commit v4 on v3

--- a/solution.py
+++ b/solution.py
@@ -116,7 +116,7 @@
     upper_ref[...] = lax.shift_right_logical(position, log2(CHUNK))
     loads[3].wait()
 
-    def chunk(c, carry):
+    for c in range(send_ref.shape[0] // WIDE):
         base = c * WIDE
         pick = jnp.concatenate(
             [lower_ref[...] * onehot(upper_ref[...] == c * GROUP + g) for g in range(GROUP)], axis=0
@@ -125,11 +125,8 @@
             iota((WIDE, devices), 0) + base == iota((WIDE, devices), 1) * block + (block - 1)
         )
         sent = matmul(pick, pep_ref[...]) + matmul(tail, meta_ref[...])
-        rows_ref[pl.ds(pl.multiple_of(base, WIDE), WIDE), :] = sent.astype(jnp.bfloat16)
+        rows_ref[base : base + WIDE, :] = sent.astype(jnp.bfloat16)
         chunk_copy(rows_ref, send_ref, sems, c).start()
-        return carry
-
-    lax.fori_loop(0, send_ref.shape[0] // WIDE, chunk, 0)
     for c in range(send_ref.shape[0] // WIDE):
         chunk_copy(rows_ref, send_ref, sems, c).wait()
 
@@ -179,42 +176,25 @@
         )
 
 
-def weights_of(logits, half_scale, half_offset, wanted, shift):
+def doubled_weights(logits, half_scale, half_offset, wanted, shift):
     hit = iota(logits.shape, 0) + shift == wanted
-    base = jnp.where(hit, -0.5, 0.5)
-    return (0.5 * jnp.tanh(logits * half_scale + half_offset) + base).astype(jnp.bfloat16)
+    base = jnp.where(hit, -1.0, 1.0)
+    return (jnp.tanh(logits * half_scale + half_offset) + base).astype(jnp.bfloat16)
 
 
 def unpack_kernel(
     block,
     odd_ref,
     got_ref,
-    spec_cross,
-    spec_own,
-    spec_partner,
     table_ref,
     slot_ref,
-    spec_ref,
     cross_ref,
     partner_ref,
     lower_ref,
-    spec_sems,
     sems,
 ):
     chunks = got_ref.shape[0] // CHUNK
-    dev_rows = SB * TILE_ROWS
     odd = odd_ref[0]
-    slots = (2 * odd, 1, 2 - 2 * odd)
-    loads = [
-        pltpu.make_async_copy(
-            spec,
-            spec_ref.at[pl.ds(pl.multiple_of(slots[n] * dev_rows, dev_rows), dev_rows)],
-            spec_sems.at[n],
-        )
-        for n, spec in enumerate((spec_cross, spec_own, spec_partner))
-    ]
-    for load in loads:
-        load.start()
 
     lane = iota((CHUNK, CHUNK), 1)
     tail = iota((CHUNK, CHUNK), 0) == lane - (lane & (block - 1)) + (block - 1)
@@ -246,11 +226,11 @@
     ]
     for store in stores:
         store.start()
-    for copy in stores + loads:
-        copy.wait()
-
-
-def unpack(odd, got, spectra, block):
+    for store in stores:
+        store.wait()
+
+
+def unpack(odd, got, block):
     slots, width = got.shape
     rows = TILE_DEV * TILE_ROWS
     chunks = slots // CHUNK
@@ -258,80 +238,110 @@
     half = pltpu.HBM((rows // 2, width), jnp.bfloat16)
     return pl.pallas_call(
         functools.partial(unpack_kernel, block),
-        in_specs=[IN_SMEM, IN_VMEM] + [ANYWHERE] * 3,
-        out_specs=[IN_VMEM] * 3 + [IN_HBM] * 2,
+        in_specs=[IN_SMEM, IN_VMEM],
+        out_specs=[IN_VMEM] * 2 + [IN_HBM] * 2,
         out_shape=[
             jax.ShapeDtypeStruct((rows, width), jnp.bfloat16),
             jax.ShapeDtypeStruct((chunks, CHUNK), jnp.int32),
-            jax.ShapeDtypeStruct((3 * SB * TILE_ROWS, width), jnp.bfloat16),
             half,
             half,
         ],
         scratch_shapes=[
             pltpu.VMEM((CHUNK, slots), jnp.bfloat16),
-            pltpu.SemaphoreType.DMA((3,)),
             pltpu.SemaphoreType.DMA((2,)),
         ],
         compiler_params=PARAMS,
         name="unpack",
-    )(odd, got, *map(in_hbm, spectra))
+    )(odd, got)
 
 
 def tiles_kernel(
     scale_ref,
     bias_ref,
+    odd_ref,
     table_ref,
     slot_ref,
-    spec_ref,
-    info_prev,
+    spec_own,
     info_own,
-    info_next,
-    band_prev,
     band_own,
-    band_next,
+    spec_cross,
+    spec_partner,
+    info_cross,
+    info_partner,
     back_ref,
     mask_ref,
     weight_ref,
     grad_ref,
+    side_ref,
+    info_ref,
+    band_ref,
     rows_ref,
+    load_sems,
     sems,
 ):
     chunks = slot_ref.shape[0]
     dev_rows = SB * TILE_ROWS
+    edge = EDGE * TILE_ROWS
     scaling = scale_ref[0] * (1.0 / math.sqrt(table_ref.shape[1]))
-    infos = (info_prev, info_own, info_next)
-    bands = (band_prev, band_own, band_next)
-
-    edge = EDGE * TILE_ROWS
-    for upper in range(TILE_DEV // EDGE):
+    odd = odd_ref[0]
+    loads = []
+    sides = [(odd, spec_cross, info_cross), (1 - odd, spec_partner, info_partner)]
+    for n, (side, spec, info) in enumerate(sides):
+        big = pl.ds(pl.multiple_of(side * dev_rows, dev_rows), dev_rows)
+        loads += [
+            pltpu.make_async_copy(spec, side_ref.at[big], load_sems.at[n, 0]),
+            pltpu.make_async_copy(info, info_ref.at[side], load_sems.at[n, 1]),
+            pltpu.make_async_copy(info, band_ref.at[side], load_sems.at[n, 2]),
+        ]
+    for load in loads:
+        load.start()
+    specs = (side_ref.at[pl.ds(0, dev_rows)], spec_own, side_ref.at[pl.ds(dev_rows, dev_rows)])
+    infos = (info_ref.at[0], info_own, info_ref.at[1])
+    bands = (band_ref.at[0], band_own, band_ref.at[1])
+
+    def weigh(upper, source):
         pair = table_ref[upper * edge : (upper + 1) * edge, :]
-        for source in (upper, upper + 1):
-            for k in range(SB):
-                first = (source * SB + k) * TILE_ROWS
-                column = first - upper * dev_rows
-                logits = matmul(pair, spec_ref[first : first + TILE_ROWS, :], ((1,), (1,)))
-                for e in range(EDGE):
-                    tag = upper * EDGE + e + (EDGE + TILE_DEV * (1 - source) + 1)
-                    place = jnp.int32(-1)
-                    for j in range(NB):
-                        place = jnp.where(bands[source][SB + k, j] == tag, j, place)
-                    active = place >= 0
-                    span = slice(e * TILE_ROWS, (e + 1) * TILE_ROWS)
-                    weight_ref[span, column : column + TILE_ROWS] = weights_of(
-                        logits[span, :],
-                        jnp.where(active, 0.5 * scaling, 0.0),
-                        jnp.where(active, 0.5 * bias_ref[0], -1e30),
-                        infos[source][k : k + 1, :],
-                        jnp.where(active, place, 2 * NB) * TILE_ROWS,
-                    )
-        total = matmul(weight_ref[...], spec_ref[upper * dev_rows : (upper + 2) * dev_rows, :])
-        grad_ref[upper * edge : (upper + 1) * edge, :] = (scaling * total).astype(jnp.bfloat16)
+        for k in range(SB):
+            column = ((source - upper) * SB + k) * TILE_ROWS
+            block = specs[source][k * TILE_ROWS : (k + 1) * TILE_ROWS, :]
+            logits = matmul(pair, block, ((1,), (1,)))
+            for e in range(EDGE):
+                tag = upper * EDGE + e + (EDGE + TILE_DEV * (1 - source) + 1)
+                place = jnp.int32(-1)
+                for j in range(NB):
+                    place = jnp.where(bands[source][SB + k, j] == tag, j, place)
+                active = place >= 0
+                span = slice(e * TILE_ROWS, (e + 1) * TILE_ROWS)
+                weight_ref[upper, span, column : column + TILE_ROWS] = doubled_weights(
+                    logits[span, :],
+                    jnp.where(active, 0.5 * scaling, 0.0),
+                    jnp.where(active, 0.5 * bias_ref[0], -1e30),
+                    infos[source][k : k + 1, :],
+                    jnp.where(active, place, 2 * NB) * TILE_ROWS,
+                )
+
+    def reduce(upper):
+        total = matmul(weight_ref[upper, :, :dev_rows], specs[upper][...])
+        total += matmul(weight_ref[upper, :, dev_rows:], specs[upper + 1][...])
+        grad_ref[upper * edge : (upper + 1) * edge, :] = (0.5 * scaling * total).astype(
+            jnp.bfloat16
+        )
+
+    weigh(0, 1)
+    weigh(1, 1)
+    for load in loads:
+        load.wait()
+    weigh(0, 0)
+    reduce(0)
+    weigh(1, 2)
+    reduce(1)
 
     def back_step(q, carry):
         for g in range(GROUP):
             columns_onehot(slot_ref[pl.ds(q * GROUP + g, 1), :], mask_ref, g * CHUNK)
+        back = matmul(mask_ref[...], grad_ref[...])
         start = pl.multiple_of(q * WIDE, WIDE)
-        rows_ref[pl.ds(start, WIDE), :] = matmul(mask_ref[...], grad_ref[...]).astype(jnp.bfloat16)
+        rows_ref[pl.ds(start, WIDE), :] = back.astype(jnp.bfloat16)
         chunk_copy(rows_ref, back_ref, sems, q).start()
         return carry
 
@@ -340,25 +350,29 @@
         chunk_copy(rows_ref, back_ref, sems, q).wait()
 
 
-def tiles(scale, bias, table, slot, spectra, infos):
+def tiles(scale, bias, odd, table, slot, spectra, info, others):
     rows, width = table.shape
     chunks = slot.shape[0]
     slots = chunks * CHUNK
     return pl.pallas_call(
         tiles_kernel,
-        in_specs=[IN_SMEM] * 2 + [IN_VMEM] * 6 + [IN_SMEM] * 3,
+        in_specs=[IN_SMEM] * 3 + [IN_VMEM] * 4 + [IN_SMEM] + [ANYWHERE] * 4,
         out_specs=IN_HBM,
         out_shape=pltpu.HBM((slots, width), jnp.bfloat16),
         scratch_shapes=[
             pltpu.VMEM((WIDE, rows), jnp.bfloat16),
-            pltpu.VMEM((EDGE * TILE_ROWS, 2 * SB * TILE_ROWS), jnp.bfloat16),
+            pltpu.VMEM((2, EDGE * TILE_ROWS, 2 * SB * TILE_ROWS), jnp.bfloat16),
             pltpu.VMEM((rows, width), jnp.bfloat16),
+            pltpu.VMEM((2 * SB * TILE_ROWS, width), jnp.bfloat16),
+            pltpu.VMEM((2, 2 * SB, TILE_ROWS), jnp.int32),
+            pltpu.SMEM((2, 2 * SB, TILE_ROWS), jnp.int32),
             pltpu.VMEM((slots, width), jnp.bfloat16),
-            pltpu.SemaphoreType.DMA((chunks,)),
+            pltpu.SemaphoreType.DMA((2, 3)),
+            pltpu.SemaphoreType.DMA((chunks // GROUP,)),
         ],
         compiler_params=PARAMS,
         name="tiles",
-    )(scale, bias, table, slot, spectra, *infos, *infos)
+    )(scale, bias, odd, table, slot, spectra, info, info, *map(in_hbm, others[:2]), *others[2:])
 
 
 def spectra_kernel(
@@ -388,7 +402,7 @@
     for j in range(NB):
         start = pl.multiple_of((band_ref[SB + k, j] - 1) * TILE_ROWS, TILE_ROWS)
         tile = ext_ref[pl.ds(start, TILE_ROWS), :]
-        weights = weights_of(
+        weights = doubled_weights(
             matmul(tile, spec_ref[...], ((1,), (1,))),
             0.5 * scaling,
             0.5 * bias_ref[0],
@@ -396,7 +410,7 @@
             j * TILE_ROWS,
         )
         total += matmul(weights, tile, ((0,), (0,)))
-    out_ref[...] = (scaling * total).astype(jnp.bfloat16)
+    out_ref[...] = (0.5 * scaling * total).astype(jnp.bfloat16)
 
 
 def spectra_gradient(scale, bias, odd, info, cross, table, partner, spectra):
@@ -429,16 +443,13 @@
 
 def home_kernel(pos_ref, got_ref, out_ref, pick_ref, grad_ref, sems):
     chunks = pos_ref.shape[0]
-
-    def chunk(c, carry):
+    for c in range(chunks // GROUP):
+        pick = pick_ref.at[c % 2]
         for g in range(GROUP):
-            columns_onehot(pos_ref[pl.ds(c * GROUP + g, 1), :], pick_ref, g * CHUNK)
-        grad = matmul(pick_ref[...], got_ref[...]).astype(jnp.bfloat16)
-        grad_ref[pl.ds(pl.multiple_of(c * WIDE, WIDE), WIDE), :] = grad
+            columns_onehot(pos_ref[c * GROUP + g : c * GROUP + g + 1, :], pick, g * CHUNK)
+        grad = matmul(pick[...], got_ref[...])
+        grad_ref[c * WIDE : (c + 1) * WIDE, :] = grad.astype(jnp.bfloat16)
         chunk_copy(grad_ref, out_ref, sems, c).start()
-        return carry
-
-    lax.fori_loop(0, chunks // GROUP, chunk, 0)
     for c in range(chunks // GROUP):
         chunk_copy(grad_ref, out_ref, sems, c).wait()
 
@@ -453,7 +464,7 @@
         out_specs=IN_HBM,
         out_shape=jax.ShapeDtypeStruct((rows, width), jnp.bfloat16),
         scratch_shapes=[
-            pltpu.VMEM((WIDE, slots), jnp.bfloat16),
+            pltpu.VMEM((2, WIDE, slots), jnp.bfloat16),
             pltpu.VMEM((rows, width), jnp.bfloat16),
             pltpu.SemaphoreType.DMA((chunks,)),
         ],
@@ -485,15 +496,14 @@
     send, position, info = pack(destination, peptides, positive, band, devices, block)
     info_cross = from_cross(info)
     info_partner = from_partner(info)
-    info_prev = jnp.where(odd == 1, info_partner, info_cross)
-    info_next = jnp.where(odd == 1, info_cross, info_partner)
     got = lax.all_to_all(send, AXES, 0, 0, tiled=True)
-    table, slot, specs, to_cross, to_partner = unpack(
-        odd, got, (spec_cross, spectra, spec_partner), block
-    )
+    table, slot, to_cross, to_partner = unpack(odd, got, block)
     cross = from_cross(to_cross)
     partner = from_partner(to_partner)
-    back = tiles(logit_scale, logit_bias, table, slot, specs, (info_prev, info, info_next))
+    back = tiles(
+        logit_scale, logit_bias, odd, table, slot, spectra, info,
+        (spec_cross, spec_partner, info_cross, info_partner),
+    )
     returned = lax.all_to_all(back, AXES, 0, 0, tiled=True)
     spec_grad = spectra_gradient(
         logit_scale, logit_bias, odd, info, cross, table, partner, spectra

time: 160 us -> 155 us (0.969)
  waiting for transfers between devices: 102 us -> 97.7 us
    ppermute x3, waiting for transfers between devices: 102 us -> 60.9 us  [from_cross(): return lax.ppermute(value, AXES, pairs + [(j, i) for i, j in pairs])]
    all_to_all x1, waiting for transfers between devices: 0.01 us -> 36.8 us  [program(): got = lax.all_to_all(send, AXES, 0, 0, tiled=True)]
  transfers between devices with their start and end apart: 8 -> 8, of which waited for: 2 -> 3; matrix products, arithmetic and copies ran while one was open for 0% -> 0% of each run, Pallas kernels for 7% -> 9%
where the time goes in v4:
time: 155 us
  waiting for transfers between devices  97.7 us (63%)
  Pallas kernels  32.8 us (21%)
  starting transfers between devices  21.1 us (14%)
  between operations  2.23 us (1%)
    ppermute x3, waiting for transfers between devices, from_cross(): return lax.ppermute(value, AXES, pairs + [(j, i) for i, j in pairs])  60.9 us
    all_to_all x1, waiting for transfers between devices, program(): got = lax.all_to_all(send, AXES, 0, 0, tiled=True)  36.8 us
    ppermute x3, starting transfers between devices, from_cross(): return lax.ppermute(value, AXES, pairs + [(j, i) for i, j in pairs])  11.5 us
    pallas_call x1, Pallas kernels, spectra_gradient(): pl.pallas_call(spectra_kernel, grid=(SB,), in_specs=[IN_SMEM, IN_SMEM, IN...  10.4 us
    pallas_call x1, Pallas kernels, tiles(): pl.pallas_call(tiles_kernel, in_specs=[IN_SMEM] * 3 + [IN_VMEM] * 4 + [IN...  10.3 us
    all_to_all x1, starting transfers between devices, program(): got = lax.all_to_all(send, AXES, 0, 0, tiled=True)  5.94 us
    pallas_call x1, Pallas kernels, pack(): pl.pallas_call(functools.partial(pack_kernel, devices, block), in_specs=[...  5.13 us
    pallas_call x1, Pallas kernels, unpack(): pl.pallas_call(functools.partial(unpack_kernel, block), in_specs=[IN_SMEM...  3.64 us
  transfers between devices with their start and end apart: 8, of which 3 were waited for; matrix products, arithmetic and copies ran while one was open for 0% of the time, Pallas kernels for 9%

profile of v4, /device:TPU:16, one launch (start us, length us, event | category | flops | bytes accessed | tf_op | source)
XLA Modules:
  0.0 155.0 jit_solution(2691124984590254815)
XLA Ops:
  0.6 5.1 %pack.1 = (bf16[2048,512]{1,0:T(8,128)(2,1)}, s32[4,256]{1,0:T(4,128)S(1)}, s32[8,256]{1,0:T(8,128)S(1)}) custom-call(s32[1,1024]{1,0:T(1,128)} %bitcast.11, bf16[1024,512]{1,0:T(8,128)(2,1)} %pep_any.1, s32[4,1,256]{2,1,0:T(1,128)} %bitcast.12, s32[4,6]{1,0:T(4,128)} %band_any.1), custom_call_target="tpu_custom_call" | custom-call | tf_op jit(solution)/shard_map/pack/pallas_call | solution.py:141
  5.8 0.0 copy-start
  5.8 5.9 %all-to-all-start = ((bf16[32,64,512]{2,1,0:T(8,128)(2,1)}), bf16[32,64,512]{2,1,0:T(8,128)(2,1)S(1)}, u32[]{:S(2)}, u32[]{:S(2)}) async-start(bf16[32,64,512]{2,1,0:T(8,128)(2,1)} %bitcast.10), calls=%async_computation | async-start | bytes 4194304 | tf_op jit(solution)/shard_map/all_to_all | solution.py:499
  11.7 0.0 copy-done
  11.7 4.0 %collective-permute-start.2 = (bf16[1024,512]{1,0:T(8,128)(2,1)S(1)}, bf16[1024,512]{1,0:T(8,128)(2,1)}, u32[]{:S(2)}, u32[]{:S(2)}) collective-permute-start(bf16[1024,512]{1,0:T(8,128)(2,1)S(1)} %copy-done), channel_id=1, source_target_pairs={{1,2},{3,4},{5,6},{7,8},{9,10},{11,12},{13,14},{15,16},{17,18},{19... | collective-permute-start | bytes 3145736 | tf_op jit(solution)/shard_map/ppermute | solution.py:484
  15.7 0.1 collective-permute-start.3
  15.8 0.5 collective-permute-start.5
  16.3 3.4 %collective-permute-start.4 = (s32[8,256]{1,0:T(8,128)S(1)}, s32[8,256]{1,0:T(8,128)S(1)}, u32[]{:S(2)}, u32[]{:S(2)}) collective-permute-start(s32[8,256]{1,0:T(8,128)S(1)} %get-tuple-element.9.band_ref.info_ref.info_own.band_own), channel_id=1, source_target_pairs={{1,2},{3,4},{5,6},{7,8},{9,10},{11,12},{13,14},{15,16},{17,18},{19... | collective-permute-start | bytes 24584 | tf_op jit(solution)/shard_map/ppermute | solution.py:484
  21.0 36.8 %all-to-all-done = bf16[32,64,512]{2,1,0:T(8,128)(2,1)S(1)} async-done(((bf16[32,64,512]{2,1,0:T(8,128)(2,1)}), bf16[32,64,512]{2,1,0:T(8,128)(2,1)S(1)}, u32[]{:S(2)}, u32[]{:S(2)}) %all-to-all-start) | async-done | bytes 2097184 | tf_op jit(solution)/shard_map/all_to_all | solution.py:499
  57.7 3.6 %unpack.1 = (bf16[1024,512]{1,0:T(8,128)(2,1)S(1)}, s32[8,256]{1,0:T(8,128)S(1)}, bf16[512,512]{1,0:T(8,128)(2,1)}, bf16[512,512]{1,0:T(8,128)(2,1)}) custom-call(s32[1]{0:T(128)} %bitcast.odd_ref, bf16[2048,512]{1,0:T(8,128)(2,1)S(1)} %bitcast.7), custom_call_target="tpu_custom_call" | custom-call | tf_op jit(solution)/shard_map/unpack/pallas_call | solution.py:239
  61.4 0.0 copy-start.1
  61.4 0.0 collective-permute-done.5.info_partner
  61.4 10.6 %collective-permute-done.4.info_cross = s32[8,256]{1,0:T(8,128)S(1)} collective-permute-done((s32[8,256]{1,0:T(8,128)S(1)}, s32[8,256]{1,0:T(8,128)S(1)}, u32[]{:S(2)}, u32[]{:S(2)}) %collective-permute-start.4) | collective-permute-done | bytes 8224 | tf_op jit(solution)/shard_map/ppermute | solution.py:484
  72.0 0.0 collective-permute-done.2.spec_cross
  72.0 0.0 collective-permute-done.3.spec_partner
  72.0 10.3 %tiles.1 = bf16[2048,512]{1,0:T(8,128)(2,1)} custom-call(f32[1]{0:T(128)S(6)} %copy.9.scale_ref, f32[1]{0:T(128)S(6)} %copy.10.bias_ref, s32[1]{0:T(128)} %bitcast.odd_ref, bf16[1024,512]{1,0:T(8,128)(2,1)S(1)} %get-tuple-element.12.own_ref.table_ref, s32[8,256]{1,0:T(8,128)S(1)} %get-tuple-element.15.slot_ref, bf16[1024,512]{1,0:T(8,128)(2,1)S(1)} %copy-done, ...), custom_call_target="tpu_custom_call" | custom-call | tf_op jit(solution)/shard_map/tiles/pallas_call | solution.py:357
  82.4 0.0 copy-done.1
  82.4 3.0 %all-to-all-start.1 = ((bf16[32,64,512]{2,1,0:T(8,128)(2,1)}), bf16[32,64,512]{2,1,0:T(8,128)(2,1)S(1)}, u32[]{:S(2)}, u32[]{:S(2)}) async-start(bf16[32,64,512]{2,1,0:T(8,128)(2,1)} %bitcast.9), calls=%async_computation.1 | async-start | bytes 4194304 | tf_op jit(solution)/shard_map/all_to_all | solution.py:507
  85.4 4.2 %collective-permute-start = (bf16[512,512]{1,0:T(8,128)(2,1)}, bf16[512,512]{1,0:T(8,128)(2,1)S(1)}, u32[]{:S(2)}, u32[]{:S(2)}) collective-permute-start(bf16[512,512]{1,0:T(8,128)(2,1)} %get-tuple-element.11), channel_id=1, source_target_pairs={{1,2},{3,4},{5,6},{7,8},{9,10},{11,12},{13,14},{15,16},{17,18},{19... | collective-permute-start | bytes 1572872 | tf_op jit(solution)/shard_map/ppermute | solution.py:484
  89.6 0.1 collective-permute-start.1
  89.7 50.2 %collective-permute-done.cross_ref = bf16[512,512]{1,0:T(8,128)(2,1)S(1)} collective-permute-done((bf16[512,512]{1,0:T(8,128)(2,1)}, bf16[512,512]{1,0:T(8,128)(2,1)S(1)}, u32[]{:S(2)}, u32[]{:S(2)}) %collective-permute-start) | collective-permute-done | bytes 524320 | tf_op jit(solution)/shard_map/ppermute | solution.py:484
  139.9 0.0 collective-permute-done.1.partner_ref
  139.9 0.0 copy-start.2
  139.9 1.2 copy-done.2
  141.2 10.4 %spectra_gradient.1 = bf16[1024,512]{1,0:T(8,128)(2,1)} custom-call(f32[1]{0:T(128)S(6)} %copy.9.scale_ref, f32[1]{0:T(128)S(6)} %copy.10.bias_ref, s32[1]{0:T(128)} %bitcast.odd_ref, s32[8,256]{1,0:T(8,128)S(1)} %get-tuple-element.9.band_ref.info_ref.info_own.band_own, bf16[512,512]{1,0:T(8,128)(2,1)S(1)} %collective-permute-done.cross_ref, ...), custom_call_target="tpu_custom_call" | custom-call | tf_op jit(solution)/shard_map/spectra_gradient/pallas_call | solution.py:419
  151.5 0.0 all-to-all-done.1
  151.6 3.3 %home.1 = bf16[1024,512]{1,0:T(8,128)(2,1)} custom-call(s32[4,256]{1,0:T(4,128)S(1)} %get-tuple-element.14.pos_ref, bf16[2048,512]{1,0:T(8,128)(2,1)S(1)} %bitcast.8), custom_call_target="tpu_custom_call" | custom-call | tf_op jit(solution)/shard_map/home/pallas_call | solution.py:461
Async XLA Ops:
  5.8 6.0 %copy-start = (bf16[1024,512]{1,0:T(8,128)(2,1)S(1)}, bf16[1024,512]{1,0:T(8,128)(2,1)}, u32[]{:S(2)}) copy-start(bf16[1024,512]{1,0:T(8,128)(2,1)} %spec_own.1) | copy-start | bytes 3145732
  5.8 52.0 %all-to-all-start = ((bf16[32,64,512]{2,1,0:T(8,128)(2,1)}), bf16[32,64,512]{2,1,0:T(8,128)(2,1)S(1)}, u32[]{:S(2)}, u32[]{:S(2)}) async-start(bf16[32,64,512]{2,1,0:T(8,128)(2,1)} %bitcast.10), calls=%async_computation | async-start | bytes 4194304 | tf_op jit(solution)/shard_map/all_to_all | solution.py:499
  11.7 60.3 %collective-permute-start.2 = (bf16[1024,512]{1,0:T(8,128)(2,1)S(1)}, bf16[1024,512]{1,0:T(8,128)(2,1)}, u32[]{:S(2)}, u32[]{:S(2)}) collective-permute-start(bf16[1024,512]{1,0:T(8,128)(2,1)S(1)} %copy-done), channel_id=1, source_target_pairs={{1,2},{3,4},{5,6},{7,8},{9,10},{11,12},{13,14},{15,16},{17,18},{19... | collective-permute-start | bytes 3145736 | tf_op jit(solution)/shard_map/ppermute | solution.py:484
  15.7 56.3 %collective-permute-start.3 = (bf16[1024,512]{1,0:T(8,128)(2,1)S(1)}, bf16[1024,512]{1,0:T(8,128)(2,1)}, u32[]{:S(2)}, u32[]{:S(2)}) collective-permute-start(bf16[1024,512]{1,0:T(8,128)(2,1)S(1)} %copy-done), channel_id=1, source_target_pairs={{0,1},{1,0},{2,3},{3,2},{4,5},{5,4},{6,7},{7,6},{8,9},{9,8},{10,11... | collective-permute-start | bytes 3145736 | tf_op jit(solution)/shard_map/ppermute | solution.py:478
  15.8 45.6 %collective-permute-start.5 = (s32[8,256]{1,0:T(8,128)S(1)}, s32[8,256]{1,0:T(8,128)S(1)}, u32[]{:S(2)}, u32[]{:S(2)}) collective-permute-start(s32[8,256]{1,0:T(8,128)S(1)} %get-tuple-element.9.band_ref.info_ref.info_own.band_own), channel_id=1, source_target_pairs={{0,1},{1,0},{2,3},{3,2},{4,5},{5,4},{6,7},{7,6},{8,9},{9,8},{10,11... | collective-permute-start | bytes 24584 | tf_op jit(solution)/shard_map/ppermute | solution.py:478
  16.3 55.7 %collective-permute-start.4 = (s32[8,256]{1,0:T(8,128)S(1)}, s32[8,256]{1,0:T(8,128)S(1)}, u32[]{:S(2)}, u32[]{:S(2)}) collective-permute-start(s32[8,256]{1,0:T(8,128)S(1)} %get-tuple-element.9.band_ref.info_ref.info_own.band_own), channel_id=1, source_target_pairs={{1,2},{3,4},{5,6},{7,8},{9,10},{11,12},{13,14},{15,16},{17,18},{19... | collective-permute-start | bytes 24584 | tf_op jit(solution)/shard_map/ppermute | solution.py:484
  61.4 21.0 %copy-start.1 = (bf16[1024,512]{1,0:T(8,128)(2,1)}, bf16[1024,512]{1,0:T(8,128)(2,1)S(1)}, u32[]{:S(2)}) copy-start(bf16[1024,512]{1,0:T(8,128)(2,1)S(1)} %get-tuple-element.12.own_ref.table_ref) | copy-start | bytes 3145732
  82.4 69.2 %all-to-all-start.1 = ((bf16[32,64,512]{2,1,0:T(8,128)(2,1)}), bf16[32,64,512]{2,1,0:T(8,128)(2,1)S(1)}, u32[]{:S(2)}, u32[]{:S(2)}) async-start(bf16[32,64,512]{2,1,0:T(8,128)(2,1)} %bitcast.9), calls=%async_computation.1 | async-start | bytes 4194304 | tf_op jit(solution)/shard_map/all_to_all | solution.py:507
  85.4 54.5 %collective-permute-start = (bf16[512,512]{1,0:T(8,128)(2,1)}, bf16[512,512]{1,0:T(8,128)(2,1)S(1)}, u32[]{:S(2)}, u32[]{:S(2)}) collective-permute-start(bf16[512,512]{1,0:T(8,128)(2,1)} %get-tuple-element.11), channel_id=1, source_target_pairs={{1,2},{3,4},{5,6},{7,8},{9,10},{11,12},{13,14},{15,16},{17,18},{19... | collective-permute-start | bytes 1572872 | tf_op jit(solution)/shard_map/ppermute | solution.py:484
  89.6 50.3 %collective-permute-start.1 = (bf16[512,512]{1,0:T(8,128)(2,1)}, bf16[512,512]{1,0:T(8,128)(2,1)S(1)}, u32[]{:S(2)}, u32[]{:S(2)}) collective-permute-start(bf16[512,512]{1,0:T(8,128)(2,1)} %get-tuple-element.13), channel_id=1, source_target_pairs={{0,1},{1,0},{2,3},{3,2},{4,5},{5,4},{6,7},{7,6},{8,9},{9,8},{10,11... | collective-permute-start | bytes 1572872 | tf_op jit(solution)/shard_map/ppermute | solution.py:478
  139.9 1.2 copy-start.2

commit v5 on v4

--- a/solution.py
+++ b/solution.py
@@ -108,10 +108,12 @@
         pos_ref[c : c + 1, :] = position[:, c * CHUNK : (c + 1) * CHUNK]
     high = lax.shift_right_logical(filled, log2(BASE))
     low = filled - high * BASE
-    lane = iota((2 * CHUNK, rows), 0)
-    part = jnp.where(lane < CHUNK, high.astype(jnp.float32), low.astype(jnp.float32))
+    lane = iota((2 * LANES, rows), 0)
+    part = jnp.where(lane < LANES, high.astype(jnp.float32), low.astype(jnp.float32))
     spread = jnp.where((lane & (block - 1)) == rank, part, 0.0).astype(jnp.bfloat16)
-    meta_ref[...] = matmul(onehot(member), spread, ((1,), (1,))).astype(jnp.bfloat16)
+    meta = matmul(onehot(member), spread, ((1,), (1,))).astype(jnp.bfloat16)
+    copies = CHUNK // LANES
+    meta_ref[...] = jnp.concatenate([meta[:, :LANES]] * copies + [meta[:, LANES:]] * copies, axis=1)
     lower_ref[...] = onehot(iota((CHUNK, rows), 0) == (position & (CHUNK - 1)))
     upper_ref[...] = lax.shift_right_logical(position, log2(CHUNK))
     loads[3].wait()
@@ -137,7 +139,7 @@
     operands = (
         destination.reshape(1, rows), peptides, positive.reshape(SB, 1, TILE_ROWS), band
     )
-    assert width == 2 * CHUNK and CHUNK % block == 0 and slots % WIDE == 0
+    assert width == 2 * CHUNK and LANES % block == 0 and slots % WIDE == 0
     return pl.pallas_call(
         functools.partial(pack_kernel, devices, block),
         in_specs=[IN_HBM] * 4,

time: 155 us -> 156 us (level)
  no operation moved by 1% of the time
where the time goes in v5:
time: 156 us; the launch traced here: 155 us
  waiting for transfers between devices  97.7 us (63%)
  Pallas kernels  33.1 us (21%)
  starting transfers between devices  21.1 us (14%)
  between operations  2.23 us (1%)
    ppermute x3, waiting for transfers between devices, from_cross(): return lax.ppermute(value, AXES, pairs + [(j, i) for i, j in pairs])  60.9 us
    all_to_all x1, waiting for transfers between devices, program(): got = lax.all_to_all(send, AXES, 0, 0, tiled=True)  36.8 us
    ppermute x3, starting transfers between devices, from_cross(): return lax.ppermute(value, AXES, pairs + [(j, i) for i, j in pairs])  11.5 us
    pallas_call x1, Pallas kernels, spectra_gradient(): pl.pallas_call(spectra_kernel, grid=(SB,), in_specs=[IN_SMEM, IN_SMEM, IN...  10.4 us
    pallas_call x1, Pallas kernels, tiles(): pl.pallas_call(tiles_kernel, in_specs=[IN_SMEM] * 3 + [IN_VMEM] * 4 + [IN...  10.3 us
    all_to_all x1, starting transfers between devices, program(): got = lax.all_to_all(send, AXES, 0, 0, tiled=True)  5.94 us
    pallas_call x1, Pallas kernels, pack(): pl.pallas_call(functools.partial(pack_kernel, devices, block), in_specs=[...  5.5 us
    pallas_call x1, Pallas kernels, unpack(): pl.pallas_call(functools.partial(unpack_kernel, block), in_specs=[IN_SMEM...  3.64 us
  transfers between devices with their start and end apart: 8, of which 3 were waited for; matrix products, arithmetic and copies ran while one was open for 0% of the time, Pallas kernels for 9%

profile of v5, /device:TPU:16, one launch (start us, length us, event | category | flops | bytes accessed | tf_op | source)
XLA Modules:
  0.0 155.4 jit_solution(6373442398023786180)
XLA Ops:
  0.6 5.5 %pack.1 = (bf16[2048,512]{1,0:T(8,128)(2,1)}, s32[4,256]{1,0:T(4,128)S(1)}, s32[8,256]{1,0:T(8,128)S(1)}) custom-call(s32[1,1024]{1,0:T(1,128)} %bitcast.11, bf16[1024,512]{1,0:T(8,128)(2,1)} %pep_any.1, s32[4,1,256]{2,1,0:T(1,128)} %bitcast.12, s32[4,6]{1,0:T(4,128)} %band_any.1), custom_call_target="tpu_custom_call" | custom-call | tf_op jit(solution)/shard_map/pack/pallas_call | solution.py:143
  6.1 0.0 copy-start
  6.2 5.9 %all-to-all-start = ((bf16[32,64,512]{2,1,0:T(8,128)(2,1)}), bf16[32,64,512]{2,1,0:T(8,128)(2,1)S(1)}, u32[]{:S(2)}, u32[]{:S(2)}) async-start(bf16[32,64,512]{2,1,0:T(8,128)(2,1)} %bitcast.10), calls=%async_computation | async-start | bytes 4194304 | tf_op jit(solution)/shard_map/all_to_all | solution.py:501
  12.1 0.0 copy-done
  12.1 4.0 %collective-permute-start.2 = (bf16[1024,512]{1,0:T(8,128)(2,1)S(1)}, bf16[1024,512]{1,0:T(8,128)(2,1)}, u32[]{:S(2)}, u32[]{:S(2)}) collective-permute-start(bf16[1024,512]{1,0:T(8,128)(2,1)S(1)} %copy-done), channel_id=1, source_target_pairs={{1,2},{3,4},{5,6},{7,8},{9,10},{11,12},{13,14},{15,16},{17,18},{19... | collective-permute-start | bytes 3145736 | tf_op jit(solution)/shard_map/ppermute | solution.py:486
  16.1 0.1 collective-permute-start.3
  16.2 0.5 collective-permute-start.5
  16.7 3.4 %collective-permute-start.4 = (s32[8,256]{1,0:T(8,128)S(1)}, s32[8,256]{1,0:T(8,128)S(1)}, u32[]{:S(2)}, u32[]{:S(2)}) collective-permute-start(s32[8,256]{1,0:T(8,128)S(1)} %get-tuple-element.9.band_ref.info_ref.info_own.band_own), channel_id=1, source_target_pairs={{1,2},{3,4},{5,6},{7,8},{9,10},{11,12},{13,14},{15,16},{17,18},{19... | collective-permute-start | bytes 24584 | tf_op jit(solution)/shard_map/ppermute | solution.py:486
  21.4 36.8 %all-to-all-done = bf16[32,64,512]{2,1,0:T(8,128)(2,1)S(1)} async-done(((bf16[32,64,512]{2,1,0:T(8,128)(2,1)}), bf16[32,64,512]{2,1,0:T(8,128)(2,1)S(1)}, u32[]{:S(2)}, u32[]{:S(2)}) %all-to-all-start) | async-done | bytes 2097184 | tf_op jit(solution)/shard_map/all_to_all | solution.py:501
  58.1 3.6 %unpack.1 = (bf16[1024,512]{1,0:T(8,128)(2,1)S(1)}, s32[8,256]{1,0:T(8,128)S(1)}, bf16[512,512]{1,0:T(8,128)(2,1)}, bf16[512,512]{1,0:T(8,128)(2,1)}) custom-call(s32[1]{0:T(128)} %bitcast.odd_ref, bf16[2048,512]{1,0:T(8,128)(2,1)S(1)} %bitcast.7), custom_call_target="tpu_custom_call" | custom-call | tf_op jit(solution)/shard_map/unpack/pallas_call | solution.py:241
  61.8 0.0 copy-start.1
  61.8 0.0 collective-permute-done.5.info_partner
  61.8 10.6 %collective-permute-done.4.info_cross = s32[8,256]{1,0:T(8,128)S(1)} collective-permute-done((s32[8,256]{1,0:T(8,128)S(1)}, s32[8,256]{1,0:T(8,128)S(1)}, u32[]{:S(2)}, u32[]{:S(2)}) %collective-permute-start.4) | collective-permute-done | bytes 8224 | tf_op jit(solution)/shard_map/ppermute | solution.py:486
  72.4 0.0 collective-permute-done.2.spec_cross
  72.4 0.0 collective-permute-done.3.spec_partner
  72.4 10.3 %tiles.1 = bf16[2048,512]{1,0:T(8,128)(2,1)} custom-call(f32[1]{0:T(128)S(6)} %copy.9.scale_ref, f32[1]{0:T(128)S(6)} %copy.10.bias_ref, s32[1]{0:T(128)} %bitcast.odd_ref, bf16[1024,512]{1,0:T(8,128)(2,1)S(1)} %get-tuple-element.12.own_ref.table_ref, s32[8,256]{1,0:T(8,128)S(1)} %get-tuple-element.15.slot_ref, bf16[1024,512]{1,0:T(8,128)(2,1)S(1)} %copy-done, ...), custom_call_target="tpu_custom_call" | custom-call | tf_op jit(solution)/shard_map/tiles/pallas_call | solution.py:359
  82.8 0.0 copy-done.1
  82.8 3.0 %all-to-all-start.1 = ((bf16[32,64,512]{2,1,0:T(8,128)(2,1)}), bf16[32,64,512]{2,1,0:T(8,128)(2,1)S(1)}, u32[]{:S(2)}, u32[]{:S(2)}) async-start(bf16[32,64,512]{2,1,0:T(8,128)(2,1)} %bitcast.9), calls=%async_computation.1 | async-start | bytes 4194304 | tf_op jit(solution)/shard_map/all_to_all | solution.py:509
  85.8 4.2 %collective-permute-start = (bf16[512,512]{1,0:T(8,128)(2,1)}, bf16[512,512]{1,0:T(8,128)(2,1)S(1)}, u32[]{:S(2)}, u32[]{:S(2)}) collective-permute-start(bf16[512,512]{1,0:T(8,128)(2,1)} %get-tuple-element.11), channel_id=1, source_target_pairs={{1,2},{3,4},{5,6},{7,8},{9,10},{11,12},{13,14},{15,16},{17,18},{19... | collective-permute-start | bytes 1572872 | tf_op jit(solution)/shard_map/ppermute | solution.py:486
  90.0 0.1 collective-permute-start.1
  90.1 50.2 %collective-permute-done.cross_ref = bf16[512,512]{1,0:T(8,128)(2,1)S(1)} collective-permute-done((bf16[512,512]{1,0:T(8,128)(2,1)}, bf16[512,512]{1,0:T(8,128)(2,1)S(1)}, u32[]{:S(2)}, u32[]{:S(2)}) %collective-permute-start) | collective-permute-done | bytes 524320 | tf_op jit(solution)/shard_map/ppermute | solution.py:486
  140.3 0.0 collective-permute-done.1.partner_ref
  140.3 0.0 copy-start.2
  140.3 1.2 copy-done.2
  141.6 10.4 %spectra_gradient.1 = bf16[1024,512]{1,0:T(8,128)(2,1)} custom-call(f32[1]{0:T(128)S(6)} %copy.9.scale_ref, f32[1]{0:T(128)S(6)} %copy.10.bias_ref, s32[1]{0:T(128)} %bitcast.odd_ref, s32[8,256]{1,0:T(8,128)S(1)} %get-tuple-element.9.band_ref.info_ref.info_own.band_own, bf16[512,512]{1,0:T(8,128)(2,1)S(1)} %collective-permute-done.cross_ref, ...), custom_call_target="tpu_custom_call" | custom-call | tf_op jit(solution)/shard_map/spectra_gradient/pallas_call | solution.py:421
  151.9 0.0 all-to-all-done.1
  151.9 3.3 %home.1 = bf16[1024,512]{1,0:T(8,128)(2,1)} custom-call(s32[4,256]{1,0:T(4,128)S(1)} %get-tuple-element.14.pos_ref, bf16[2048,512]{1,0:T(8,128)(2,1)S(1)} %bitcast.8), custom_call_target="tpu_custom_call" | custom-call | tf_op jit(solution)/shard_map/home/pallas_call | solution.py:463
Async XLA Ops:
  6.1 6.0 %copy-start = (bf16[1024,512]{1,0:T(8,128)(2,1)S(1)}, bf16[1024,512]{1,0:T(8,128)(2,1)}, u32[]{:S(2)}) copy-start(bf16[1024,512]{1,0:T(8,128)(2,1)} %spec_own.1) | copy-start | bytes 3145732
  6.2 52.0 %all-to-all-start = ((bf16[32,64,512]{2,1,0:T(8,128)(2,1)}), bf16[32,64,512]{2,1,0:T(8,128)(2,1)S(1)}, u32[]{:S(2)}, u32[]{:S(2)}) async-start(bf16[32,64,512]{2,1,0:T(8,128)(2,1)} %bitcast.10), calls=%async_computation | async-start | bytes 4194304 | tf_op jit(solution)/shard_map/all_to_all | solution.py:501
  12.1 60.3 %collective-permute-start.2 = (bf16[1024,512]{1,0:T(8,128)(2,1)S(1)}, bf16[1024,512]{1,0:T(8,128)(2,1)}, u32[]{:S(2)}, u32[]{:S(2)}) collective-permute-start(bf16[1024,512]{1,0:T(8,128)(2,1)S(1)} %copy-done), channel_id=1, source_target_pairs={{1,2},{3,4},{5,6},{7,8},{9,10},{11,12},{13,14},{15,16},{17,18},{19... | collective-permute-start | bytes 3145736 | tf_op jit(solution)/shard_map/ppermute | solution.py:486
  16.1 56.3 %collective-permute-start.3 = (bf16[1024,512]{1,0:T(8,128)(2,1)S(1)}, bf16[1024,512]{1,0:T(8,128)(2,1)}, u32[]{:S(2)}, u32[]{:S(2)}) collective-permute-start(bf16[1024,512]{1,0:T(8,128)(2,1)S(1)} %copy-done), channel_id=1, source_target_pairs={{0,1},{1,0},{2,3},{3,2},{4,5},{5,4},{6,7},{7,6},{8,9},{9,8},{10,11... | collective-permute-start | bytes 3145736 | tf_op jit(solution)/shard_map/ppermute | solution.py:480
  16.2 45.6 %collective-permute-start.5 = (s32[8,256]{1,0:T(8,128)S(1)}, s32[8,256]{1,0:T(8,128)S(1)}, u32[]{:S(2)}, u32[]{:S(2)}) collective-permute-start(s32[8,256]{1,0:T(8,128)S(1)} %get-tuple-element.9.band_ref.info_ref.info_own.band_own), channel_id=1, source_target_pairs={{0,1},{1,0},{2,3},{3,2},{4,5},{5,4},{6,7},{7,6},{8,9},{9,8},{10,11... | collective-permute-start | bytes 24584 | tf_op jit(solution)/shard_map/ppermute | solution.py:480
  16.7 55.7 %collective-permute-start.4 = (s32[8,256]{1,0:T(8,128)S(1)}, s32[8,256]{1,0:T(8,128)S(1)}, u32[]{:S(2)}, u32[]{:S(2)}) collective-permute-start(s32[8,256]{1,0:T(8,128)S(1)} %get-tuple-element.9.band_ref.info_ref.info_own.band_own), channel_id=1, source_target_pairs={{1,2},{3,4},{5,6},{7,8},{9,10},{11,12},{13,14},{15,16},{17,18},{19... | collective-permute-start | bytes 24584 | tf_op jit(solution)/shard_map/ppermute | solution.py:486
  61.8 21.0 %copy-start.1 = (bf16[1024,512]{1,0:T(8,128)(2,1)}, bf16[1024,512]{1,0:T(8,128)(2,1)S(1)}, u32[]{:S(2)}) copy-start(bf16[1024,512]{1,0:T(8,128)(2,1)S(1)} %get-tuple-element.12.own_ref.table_ref) | copy-start | bytes 3145732
  82.8 69.2 %all-to-all-start.1 = ((bf16[32,64,512]{2,1,0:T(8,128)(2,1)}), bf16[32,64,512]{2,1,0:T(8,128)(2,1)S(1)}, u32[]{:S(2)}, u32[]{:S(2)}) async-start(bf16[32,64,512]{2,1,0:T(8,128)(2,1)} %bitcast.9), calls=%async_computation.1 | async-start | bytes 4194304 | tf_op jit(solution)/shard_map/all_to_all | solution.py:509
  85.8 54.5 %collective-permute-start = (bf16[512,512]{1,0:T(8,128)(2,1)}, bf16[512,512]{1,0:T(8,128)(2,1)S(1)}, u32[]{:S(2)}, u32[]{:S(2)}) collective-permute-start(bf16[512,512]{1,0:T(8,128)(2,1)} %get-tuple-element.11), channel_id=1, source_target_pairs={{1,2},{3,4},{5,6},{7,8},{9,10},{11,12},{13,14},{15,16},{17,18},{19... | collective-permute-start | bytes 1572872 | tf_op jit(solution)/shard_map/ppermute | solution.py:486
  90.0 50.3 %collective-permute-start.1 = (bf16[512,512]{1,0:T(8,128)(2,1)}, bf16[512,512]{1,0:T(8,128)(2,1)S(1)}, u32[]{:S(2)}, u32[]{:S(2)}) collective-permute-start(bf16[512,512]{1,0:T(8,128)(2,1)} %get-tuple-element.13), channel_id=1, source_target_pairs={{0,1},{1,0},{2,3},{3,2},{4,5},{5,4},{6,7},{7,6},{8,9},{9,8},{10,11... | collective-permute-start | bytes 1572872 | tf_op jit(solution)/shard_map/ppermute | solution.py:480
  140.3 1.2 copy-start.2
